TPU v7x, 256 devices: a whole 4x4x8 slice. The times are simulated.
256 devices in a mesh: group: 64 (over z, x, core), local: 4 (over y).
Axes of the slice: x: 4, y: 4, z: 8, core: 2. Of those that a mesh axis runs over, the one named last changes fastest.
Arguments:
- tokens: bfloat16 [16384, 3584], P(('group', 'local')), may hold values from -6 to 6
- expert_ids: int32 [16384, 8], P(('group', 'local')), may hold values from -1 to 127, as said below
- gate_weights: float32 [16384, 8], P(('group', 'local')), may hold values from 0.05 to 1
- w_gate: bfloat16 [3584, 131072], P(None, ('group', 'local')), may hold values from -0.09375 to 0.09375
- w_up: bfloat16 [3584, 131072], P(None, ('group', 'local')), may hold values from -0.09375 to 0.09375
- w_down: bfloat16 [131072, 3584], P(('group', 'local')), may hold values from -0.1875 to 0.1875
Outputs:
- moe_output: bfloat16 [16384, 3584], P(('group', 'local'))
Inputs may be any that keep to these rules, and one draw needn't show every extreme that they name: `expert_ids`: each row names up to 8 different experts (the other entries are -1): one or two in each of at most 4 groups. At most 16 rows of one device name experts of one group, and in every draw some group is named by exactly 16 rows of every device.
All inputs are finite; a program needn't handle non-finite values.
Results may differ from a plain program's by a relative error of at most 0.012.
Values may be sent and summed in bfloat16 or wider, within the bound.
A program may use at most 128 MiB of HBM per device.

v0:
```python
import jax
import jax.numpy as jnp
from jax import lax
from jax.sharding import PartitionSpec as P

N_CHUNK = 2


def shifted(array, shift):
    n_local = lax.axis_size("local")
    return lax.ppermute(array, "local", [(i, (i + shift) % n_local) for i in range(n_local)])


def one_hot_dot(select, values, spec):
    return jnp.einsum(spec, select, values, preferred_element_type=jnp.float32).astype(jnp.bfloat16)


def local(tokens, expert_ids, gate_weights, w_gate, w_up, w_down):
    n_groups = lax.axis_size("group")
    n_local = lax.axis_size("local")
    per_group = n_local // 2
    tok_rows, width = tokens.shape
    chunk = width // N_CHUNK
    send_cap = tok_rows // 4
    expert_cap = n_groups * send_cap * 5 // 16
    expert_count = n_groups * per_group
    arrived_count = n_groups * send_cap
    expert_line = jnp.arange(expert_count, dtype=jnp.int32)
    hit_table = expert_ids[:, :, None] == expert_line
    named = jnp.any(hit_table, axis=1).reshape(tok_rows, n_groups, per_group)
    gate_table = jnp.sum(jnp.where(hit_table, gate_weights[:, :, None], 0.0), axis=1)
    gate_table = gate_table.reshape(tok_rows, n_groups, per_group)
    chosen = jnp.any(named, axis=2)
    send_slot = jnp.cumsum(chosen.astype(jnp.int32), axis=0) - 1
    slot_line = jnp.arange(send_cap, dtype=jnp.int32)
    token_line = jnp.arange(tok_rows, dtype=jnp.int32)
    group_line = jnp.arange(n_groups, dtype=jnp.int32)
    match_send = chosen[:, :, None] & (send_slot[:, :, None] == slot_line)
    source_row = jnp.sum(jnp.where(match_send, token_line[:, None, None], 0), axis=0)
    send_used = jnp.any(match_send, axis=0)
    gates_out = jnp.where(send_used[:, :, None], gate_table[source_row, group_line[:, None]], 0.0)
    flags_out = (send_used[:, :, None] & named[source_row, group_line[:, None]]).astype(jnp.float32)
    meta_out = jnp.concatenate([gates_out, flags_out], axis=2)
    meta_in = lax.all_to_all(meta_out, "group", split_axis=0, concat_axis=0, tiled=True)
    meta_in = meta_in.reshape(arrived_count, 2 * per_group)
    arrived_gates = meta_in[:, :per_group]
    wanted = meta_in[:, per_group:] > 0.5
    arrive_rank = jnp.cumsum(wanted.astype(jnp.int32), axis=0) - 1
    taken = wanted & (arrive_rank < expert_cap)
    cap_line = jnp.arange(expert_cap, dtype=jnp.int32)
    match_expert = taken[:, :, None] & (arrive_rank[:, :, None] == cap_line)
    expert_gates = jnp.sum(jnp.where(match_expert, arrived_gates[:, :, None], 0.0), axis=0)
    pick = match_expert.reshape(arrived_count, per_group * expert_cap).astype(jnp.bfloat16)
    send_select = match_send.reshape(tok_rows, arrived_count).astype(jnp.bfloat16)
    here = lax.axis_index("local")
    device_line = jnp.arange(n_local, dtype=jnp.int32)

    gate_acc = None
    up_acc = None
    for c in range(N_CHUNK):
        cols = slice(c * chunk, (c + 1) * chunk)
        rows_out = one_hot_dot(send_select, tokens[:, cols], "tk,td->kd")
        rows_in = lax.all_to_all(
            rows_out.reshape(n_groups, send_cap, chunk), "group", split_axis=0, concat_axis=0, tiled=True
        ).reshape(arrived_count, chunk)
        expert_rows = one_hot_dot(pick, rows_in, "ak,ad->kd").reshape(per_group, expert_cap, chunk)
        blocks = []
        for shift in range(n_local):
            dest_expert = ((here + shift) % n_local) // 2
            block = lax.dynamic_index_in_dim(expert_rows, dest_expert, 0, keepdims=False)
            blocks.append(block if shift == 0 else shifted(block, shift))
        flat_rows = jnp.concatenate(blocks, axis=0)
        g_part = jnp.dot(flat_rows, w_gate[cols, :], preferred_element_type=jnp.float32)
        u_part = jnp.dot(flat_rows, w_up[cols, :], preferred_element_type=jnp.float32)
        gate_acc = g_part if gate_acc is None else gate_acc + g_part
        up_acc = u_part if up_acc is None else up_acc + u_part
    hidden = (jax.nn.silu(gate_acc) * up_acc).astype(jnp.bfloat16)

    outs = []
    owner = ((here + device_line) % n_local) // 2 == jnp.arange(per_group, dtype=jnp.int32)[:, None]
    for c in range(N_CHUNK):
        cols = slice(c * chunk, (c + 1) * chunk)
        partial_value = jnp.dot(hidden, w_down[:, cols], preferred_element_type=jnp.float32)
        partial_value = partial_value.astype(jnp.bfloat16).reshape(n_local, expert_cap, chunk)
        by_shift = [partial_value[0]] + [
            shifted(partial_value[shift], (n_local - shift) % n_local) for shift in range(1, n_local)
        ]
        stacked, owner_c, gates_c, pick_c = lax.optimization_barrier((jnp.stack(by_shift), owner, expert_gates, pick))
        summed = jnp.sum(jnp.where(owner_c[:, :, None, None], stacked.astype(jnp.float32)[None], 0.0), axis=1)
        term = (gates_c[:, :, None] * summed).astype(jnp.bfloat16)
        group_part = one_hot_dot(pick_c, term.reshape(per_group * expert_cap, chunk), "ak,kd->ad")
        back = lax.all_to_all(
            group_part.reshape(n_groups, send_cap, chunk), "group", split_axis=0, concat_axis=0, tiled=True
        ).reshape(arrived_count, chunk)
        outs.append(one_hot_dot(send_select, back, "tk,kd->td"))
    return jnp.concatenate(outs, axis=1)


def solution(mesh):
    in_specs = (
        P(("group", "local"), None),
        P(("group", "local"), None),
        P(("group", "local"), None),
        P(None, ("group", "local")),
        P(None, ("group", "local")),
        P(("group", "local"), None),
    )
    out_specs = P(("group", "local"), None)

    return jax.shard_map(local, mesh=mesh, in_specs=in_specs, out_specs=out_specs, check_vma=False)
```

profile of v0, /device:TPU:1, one launch (start us, length us, event | category | flops | bytes accessed | tf_op | source)
XLA Modules:
  0.0 557.5 jit_solution(12176092708741195631)
XLA Ops:
  1.1 1.9 copy.68
  6.0 5.7 %gather_fusion.1 = pred[1024,2]{1,0:T(8,128)(4,1)S(1)} fusion(pred[64,64,2]{2,1,0:T(8,128)(4,1)S(1)} %copy.68, s32[1024]{0:T(1024)S(1)} %reshape.218), kind=kCustom, calls=%fused_computation.1 | custom fusion | bytes 12288 | tf_op jit(solution)/shard_map/gather | solution.py:42
  12.5 1.9 copy.66
  14.4 6.8 %gather_fusion = f32[1024,2]{1,0:T(8,128)S(1)} fusion(f32[64,64,2]{2,1,0:T(8,128)S(1)} %copy.66, s32[1024]{0:T(1024)S(1)} %reshape.218), kind=kCustom, calls=%fused_computation | custom fusion | bytes 24576 | tf_op jit(solution)/shard_map/gather | solution.py:41
  22.3 13.0 %all-to-all-start = ((f32[64,16,4]{1,2,0:T(4,128)}), f32[64,16,4]{1,2,0:T(4,128)S(1)}, u32[]{:S(2)}, u32[]{:S(2)}) async-start(f32[64,16,4]{1,2,0:T(4,128)} %copy.70), calls=%async_computation | async-start | bytes 262144 | tf_op jit(solution)/shard_map/all_to_all | solution.py:44
  35.6 2.9 convolution_convert_fusion.4
  38.5 7.8 %all-to-all-done = f32[64,16,4]{1,2,0:T(4,128)S(1)} async-done(((f32[64,16,4]{1,2,0:T(4,128)}), f32[64,16,4]{1,2,0:T(4,128)S(1)}, u32[]{:S(2)}, u32[]{:S(2)}) %all-to-all-start) | async-done | bytes 16416 | tf_op jit(solution)/shard_map/all_to_all | solution.py:44
  46.4 5.4 all-to-all-start.2
  51.8 2.9 convolution_convert_fusion.5
  54.6 81.0 %all-to-all-done.2 = bf16[64,16,1792]{2,1,0:T(8,128)(2,1)} async-done(((bf16[64,16,1792]{2,1,0:T(8,128)(2,1)}), bf16[64,16,1792]{2,1,0:T(8,128)(2,1)}, u32[]{:S(2)}, u32[]{:S(2)}) %all-to-all-start.2) | async-done | bytes 3670048 | tf_op jit(solution)/shard_map/all_to_all | solution.py:63
  135.7 7.2 %all-to-all-start.1 = ((bf16[64,16,1792]{2,1,0:T(8,128)(2,1)}), bf16[64,16,1792]{2,1,0:T(8,128)(2,1)}, u32[]{:S(2)}, u32[]{:S(2)}) async-start(bf16[64,16,1792]{2,1,0:T(8,128)(2,1)} %bitcast.109), calls=%async_computation.1 | async-start | bytes 7340032 | tf_op jit(solution)/shard_map/all_to_all | solution.py:63
  144.7 4.6 convolution_convert_fusion.6
  149.3 1.8 dynamic-slice_bitcast_fusion.3
  152.4 2.6 collective-permute-start.4
  156.1 70.5 %all-to-all-done.1 = bf16[64,16,1792]{2,1,0:T(8,128)(2,1)} async-done(((bf16[64,16,1792]{2,1,0:T(8,128)(2,1)}), bf16[64,16,1792]{2,1,0:T(8,128)(2,1)}, u32[]{:S(2)}, u32[]{:S(2)}) %all-to-all-start.1) | async-done | bytes 3670048 | tf_op jit(solution)/shard_map/all_to_all | solution.py:63
  226.6 4.6 convolution_convert_fusion.7
  231.5 1.4 collective-permute-start
  232.9 2.6 collective-permute-start.1
  236.8 5.3 fusion.9
  242.1 5.1 fusion.14
  247.3 10.6 %collective-permute-done = bf16[320,1792]{1,0:T(8,128)(2,1)S(1)} collective-permute-done((bf16[320,1792]{1,0:T(8,128)(2,1)S(1)}, bf16[320,1792]{1,0:T(8,128)(2,1)S(1)}, u32[]{:S(2)}, u32[]{:S(2)}) %collective-permute-start) | collective-permute-done | bytes 1146912 | tf_op jit(solution)/shard_map/ppermute | solution.py:11
  257.8 25.7 %collective-permute-done.1 = bf16[320,1792]{1,0:T(8,128)(2,1)S(1)} collective-permute-done((bf16[320,1792]{1,0:T(8,128)(2,1)S(1)}, bf16[320,1792]{1,0:T(8,128)(2,1)S(1)}, u32[]{:S(2)}, u32[]{:S(2)}) %collective-permute-start.1) | collective-permute-done | bytes 1146912 | tf_op jit(solution)/shard_map/ppermute | solution.py:11
  284.3 2.5 convolution_add_fusion.1
  286.8 2.9 multiply_convert_fusion
  289.8 2.5 convolution_convert_fusion.1
  292.3 1.8 slice_bitcast_fusion.1
  294.2 3.4 collective-permute-start.6
  299.8 46.7 %collective-permute-done.6 = bf16[320,1792]{1,0:T(8,128)(2,1)} collective-permute-done((bf16[320,1792]{1,0:T(8,128)(2,1)}, bf16[320,1792]{1,0:T(8,128)(2,1)}, u32[]{:S(2)}, u32[]{:S(2)}) %collective-permute-start.6) | collective-permute-done | bytes 1146912 | tf_op jit(solution)/shard_map/ppermute | solution.py:11
  346.5 4.7 collective-permute-done.8
  351.2 2.2 pad_maximum_fusion.2
  353.4 4.3 convert_element_type.71
  357.8 7.6 %select_reduce_fusion.1 = f32[2,320,1792]{2,1,0:T(8,128)} fusion(f32[4,320,1792]{2,1,0:T(8,128)} %convert_element_type.71, pred[2,4]{1,0:T(4,128)(4,1)S(1)} %iota_compare_fusion.3), kind=kLoop, calls=%fused_computation.3 | loop fusion | flops 8028160 | bytes 13762568 | tf_op jit(solution)/shard_map/reduce_sum | solution.py:89
  365.4 2.6 fusion.1
  368.0 4.5 convolution_convert_fusion.3
  372.5 6.7 %all-to-all-start.3 = ((bf16[64,16,1792]{2,1,0:T(8,128)(2,1)}), bf16[64,16,1792]{2,1,0:T(8,128)(2,1)}, u32[]{:S(2)}, u32[]{:S(2)}) async-start(bf16[64,16,1792]{2,1,0:T(8,128)(2,1)} %bitcast.113), calls=%async_computation.3 | async-start | bytes 7340032 | tf_op jit(solution)/shard_map/all_to_all | solution.py:92
  379.2 4.4 convolution_convert_fusion
  385.7 24.8 %collective-permute-done.9 = bf16[320,1792]{1,0:T(8,128)(2,1)S(1)} collective-permute-done((bf16[320,1792]{1,0:T(8,128)(2,1)S(1)}, bf16[320,1792]{1,0:T(8,128)(2,1)S(1)}, u32[]{:S(2)}, u32[]{:S(2)}) %collective-permute-start.9) | collective-permute-done | bytes 1146912 | tf_op jit(solution)/shard_map/ppermute | solution.py:11
  410.4 1.6 collective-permute-done.10
  412.0 25.7 %collective-permute-done.11 = bf16[320,1792]{1,0:T(8,128)(2,1)S(1)} collective-permute-done((bf16[320,1792]{1,0:T(8,128)(2,1)S(1)}, bf16[320,1792]{1,0:T(8,128)(2,1)S(1)}, u32[]{:S(2)}, u32[]{:S(2)}) %collective-permute-start.11) | collective-permute-done | bytes 1146912 | tf_op jit(solution)/shard_map/ppermute | solution.py:11
  438.3 4.3 convert_element_type.76
  442.7 7.6 %select_reduce_fusion = f32[2,320,1792]{2,1,0:T(8,128)} fusion(f32[4,320,1792]{2,1,0:T(8,128)} %convert_element_type.76, pred[2,4]{1,0:T(4,128)(4,1)S(1)} %iota_compare_fusion.3), kind=kLoop, calls=%fused_computation.2 | loop fusion | flops 8028160 | bytes 13762568 | tf_op jit(solution)/shard_map/reduce_sum | solution.py:89
  450.4 2.6 fusion
  453.0 4.5 convolution_convert_fusion.2
  457.5 5.3 all-to-all-done.3
  462.8 6.9 %all-to-all-start.4 = ((bf16[64,16,1792]{2,1,0:T(8,128)(2,1)}), bf16[64,16,1792]{2,1,0:T(8,128)(2,1)}, u32[]{:S(2)}, u32[]{:S(2)}) async-start(bf16[64,16,1792]{2,1,0:T(8,128)(2,1)} %bitcast.114), calls=%async_computation.4 | async-start | bytes 7340032 | tf_op jit(solution)/shard_map/all_to_all | solution.py:92
  469.8 2.8 fusion.5
  472.6 81.1 %all-to-all-done.4 = bf16[64,16,1792]{2,1,0:T(8,128)(2,1)} async-done(((bf16[64,16,1792]{2,1,0:T(8,128)(2,1)}), bf16[64,16,1792]{2,1,0:T(8,128)(2,1)}, u32[]{:S(2)}, u32[]{:S(2)}) %all-to-all-start.4) | async-done | bytes 3670048 | tf_op jit(solution)/shard_map/all_to_all | solution.py:92
  553.7 2.8 fusion.6
  (78 shorter events, 18.3 us)
Async XLA Ops:
  0.0 12.1 %copy-start.1 = (f32[64,8]{0,1:T(8,128)S(1)}, f32[64,8]{0,1:T(8,128)}, u32[]{:S(2)}) copy-start(f32[64,8]{0,1:T(8,128)} %param.8) | copy-start | bytes 6148
  14.4 21.2 %copy-start = (bf16[64,3584]{1,0:T(8,128)(2,1)S(1)}, bf16[64,3584]{1,0:T(8,128)(2,1)}, u32[]{:S(2)}) copy-start(bf16[64,3584]{1,0:T(8,128)(2,1)} %param.6) | copy-start | bytes 1376260
  22.3 24.1 %all-to-all-start = ((f32[64,16,4]{1,2,0:T(4,128)}), f32[64,16,4]{1,2,0:T(4,128)S(1)}, u32[]{:S(2)}, u32[]{:S(2)}) async-start(f32[64,16,4]{1,2,0:T(4,128)} %copy.70), calls=%async_computation | async-start | bytes 262144 | tf_op jit(solution)/shard_map/all_to_all | solution.py:44
  46.4 89.3 %all-to-all-start.2 = ((bf16[64,16,1792]{2,1,0:T(8,128)(2,1)}), bf16[64,16,1792]{2,1,0:T(8,128)(2,1)}, u32[]{:S(2)}, u32[]{:S(2)}) async-start(bf16[64,16,1792]{2,1,0:T(8,128)(2,1)} %bitcast.110), calls=%async_computation.2 | async-start | bytes 7340032 | tf_op jit(solution)/shard_map/all_to_all | solution.py:63
  135.7 90.9 %all-to-all-start.1 = ((bf16[64,16,1792]{2,1,0:T(8,128)(2,1)}), bf16[64,16,1792]{2,1,0:T(8,128)(2,1)}, u32[]{:S(2)}, u32[]{:S(2)}) async-start(bf16[64,16,1792]{2,1,0:T(8,128)(2,1)} %bitcast.109), calls=%async_computation.1 | async-start | bytes 7340032 | tf_op jit(solution)/shard_map/all_to_all | solution.py:63
  151.1 84.4 %collective-permute-start.3 = (bf16[320,1792]{1,0:T(8,128)(2,1)}, bf16[320,1792]{1,0:T(8,128)(2,1)}, u32[]{:S(2)}, u32[]{:S(2)}) collective-permute-start(bf16[320,1792]{1,0:T(8,128)(2,1)} %get-tuple-element.36), channel_id=1, source_target_pairs={{0,1},{1,2},{2,3},{3,0},{4,5},{5,6},{6,7},{7,4},{8,9},{9,10},{10,1... | collective-permute-start | bytes 3440648 | tf_op jit(solution)/shard_map/ppermute | solution.py:11
  152.4 84.4 %collective-permute-start.4 = (bf16[320,1792]{1,0:T(8,128)(2,1)}, bf16[320,1792]{1,0:T(8,128)(2,1)}, u32[]{:S(2)}, u32[]{:S(2)}) collective-permute-start(bf16[320,1792]{1,0:T(8,128)(2,1)} %get-tuple-element.35), channel_id=1, source_target_pairs={{0,2},{1,3},{2,0},{3,1},{4,6},{5,7},{6,4},{7,5},{8,10},{9,11},{10,... | collective-permute-start | bytes 3440648 | tf_op jit(solution)/shard_map/ppermute | solution.py:11
  155.0 81.8 %collective-permute-start.5 = (bf16[320,1792]{1,0:T(8,128)(2,1)S(1)}, bf16[320,1792]{1,0:T(8,128)(2,1)}, u32[]{:S(2)}, u32[]{:S(2)}) collective-permute-start(bf16[320,1792]{1,0:T(8,128)(2,1)S(1)} %get-tuple-element.34), channel_id=1, source_target_pairs={{0,3},{1,0},{2,1},{3,2},{4,7},{5,4},{6,5},{7,6},{8,11},{9,8},{10,9... | collective-permute-start | bytes 3440648 | tf_op jit(solution)/shard_map/ppermute | solution.py:11
  231.2 5.6 %copy-start.3 = (bf16[3584,512]{1,0:T(8,128)(2,1)S(1)}, bf16[3584,512]{1,0:T(8,128)(2,1)}, u32[]{:S(2)}) copy-start(bf16[3584,512]{1,0:T(8,128)(2,1)} %param.10) | copy-start | bytes 11010052
  231.5 26.3 %collective-permute-start = (bf16[320,1792]{1,0:T(8,128)(2,1)S(1)}, bf16[320,1792]{1,0:T(8,128)(2,1)S(1)}, u32[]{:S(2)}, u32[]{:S(2)}) collective-permute-start(bf16[320,1792]{1,0:T(8,128)(2,1)S(1)} %get-tuple-element.32), channel_id=1, source_target_pairs={{0,1},{1,2},{2,3},{3,0},{4,5},{5,6},{6,7},{7,4},{8,9},{9,10},{10,1... | collective-permute-start | bytes 3440648 | tf_op jit(solution)/shard_map/ppermute | solution.py:11
  232.9 50.6 %collective-permute-start.1 = (bf16[320,1792]{1,0:T(8,128)(2,1)S(1)}, bf16[320,1792]{1,0:T(8,128)(2,1)S(1)}, u32[]{:S(2)}, u32[]{:S(2)}) collective-permute-start(bf16[320,1792]{1,0:T(8,128)(2,1)S(1)} %get-tuple-element.31), channel_id=1, source_target_pairs={{0,2},{1,3},{2,0},{3,1},{4,6},{5,7},{6,4},{7,5},{8,10},{9,11},{10,... | collective-permute-start | bytes 3440648 | tf_op jit(solution)/shard_map/ppermute | solution.py:11
  235.5 48.8 %collective-permute-start.2 = (bf16[320,1792]{1,0:T(8,128)(2,1)S(1)}, bf16[320,1792]{1,0:T(8,128)(2,1)S(1)}, u32[]{:S(2)}, u32[]{:S(2)}) collective-permute-start(bf16[320,1792]{1,0:T(8,128)(2,1)S(1)} %get-tuple-element.30), channel_id=1, source_target_pairs={{0,3},{1,0},{2,1},{3,2},{4,7},{5,4},{6,5},{7,6},{8,11},{9,8},{10,9... | collective-permute-start | bytes 3440648 | tf_op jit(solution)/shard_map/ppermute | solution.py:11
  236.8 5.3 copy-start.2
  286.8 2.9 copy-start.4
  289.7 2.6 copy-start.5
  294.2 52.3 %collective-permute-start.6 = (bf16[320,1792]{1,0:T(8,128)(2,1)}, bf16[320,1792]{1,0:T(8,128)(2,1)}, u32[]{:S(2)}, u32[]{:S(2)}) collective-permute-start(bf16[320,1792]{1,0:T(8,128)(2,1)} %get-tuple-element.24), channel_id=1, source_target_pairs={{0,3},{1,0},{2,1},{3,2},{4,7},{5,4},{6,5},{7,6},{8,11},{9,8},{10,9... | collective-permute-start | bytes 3440648 | tf_op jit(solution)/shard_map/ppermute | solution.py:11
  297.6 48.9 %collective-permute-start.7 = (bf16[320,1792]{1,0:T(8,128)(2,1)}, bf16[320,1792]{1,0:T(8,128)(2,1)}, u32[]{:S(2)}, u32[]{:S(2)}) collective-permute-start(bf16[320,1792]{1,0:T(8,128)(2,1)} %get-tuple-element.23), channel_id=1, source_target_pairs={{0,2},{1,3},{2,0},{3,1},{4,6},{5,7},{6,4},{7,5},{8,10},{9,11},{10,... | collective-permute-start | bytes 3440648 | tf_op jit(solution)/shard_map/ppermute | solution.py:11
  298.1 53.0 %collective-permute-start.8 = (bf16[320,1792]{1,0:T(8,128)(2,1)}, bf16[320,1792]{1,0:T(8,128)(2,1)}, u32[]{:S(2)}, u32[]{:S(2)}) collective-permute-start(bf16[320,1792]{1,0:T(8,128)(2,1)} %get-tuple-element.22), channel_id=1, source_target_pairs={{0,1},{1,2},{2,3},{3,0},{4,5},{5,6},{6,7},{7,4},{8,9},{9,10},{10,1... | collective-permute-start | bytes 3440648 | tf_op jit(solution)/shard_map/ppermute | solution.py:11
  372.5 90.3 %all-to-all-start.3 = ((bf16[64,16,1792]{2,1,0:T(8,128)(2,1)}), bf16[64,16,1792]{2,1,0:T(8,128)(2,1)}, u32[]{:S(2)}, u32[]{:S(2)}) async-start(bf16[64,16,1792]{2,1,0:T(8,128)(2,1)} %bitcast.113), calls=%async_computation.3 | async-start | bytes 7340032 | tf_op jit(solution)/shard_map/all_to_all | solution.py:92
  384.0 26.5 %collective-permute-start.9 = (bf16[320,1792]{1,0:T(8,128)(2,1)S(1)}, bf16[320,1792]{1,0:T(8,128)(2,1)S(1)}, u32[]{:S(2)}, u32[]{:S(2)}) collective-permute-start(bf16[320,1792]{1,0:T(8,128)(2,1)S(1)} %get-tuple-element.28), channel_id=1, source_target_pairs={{0,3},{1,0},{2,1},{3,2},{4,7},{5,4},{6,5},{7,6},{8,11},{9,8},{10,9... | collective-permute-start | bytes 3440648 | tf_op jit(solution)/shard_map/ppermute | solution.py:11
  384.4 27.7 %collective-permute-start.10 = (bf16[320,1792]{1,0:T(8,128)(2,1)S(1)}, bf16[320,1792]{1,0:T(8,128)(2,1)S(1)}, u32[]{:S(2)}, u32[]{:S(2)}) collective-permute-start(bf16[320,1792]{1,0:T(8,128)(2,1)S(1)} %get-tuple-element.27), channel_id=1, source_target_pairs={{0,2},{1,3},{2,0},{3,1},{4,6},{5,7},{6,4},{7,5},{8,10},{9,11},{10,... | collective-permute-start | bytes 3440648 | tf_op jit(solution)/shard_map/ppermute | solution.py:11
  384.9 52.8 %collective-permute-start.11 = (bf16[320,1792]{1,0:T(8,128)(2,1)S(1)}, bf16[320,1792]{1,0:T(8,128)(2,1)S(1)}, u32[]{:S(2)}, u32[]{:S(2)}) collective-permute-start(bf16[320,1792]{1,0:T(8,128)(2,1)S(1)} %get-tuple-element.26), channel_id=1, source_target_pairs={{0,1},{1,2},{2,3},{3,0},{4,5},{5,6},{6,7},{7,4},{8,9},{9,10},{10,1... | collective-permute-start | bytes 3440648 | tf_op jit(solution)/shard_map/ppermute | solution.py:11
  462.8 90.9 %all-to-all-start.4 = ((bf16[64,16,1792]{2,1,0:T(8,128)(2,1)}), bf16[64,16,1792]{2,1,0:T(8,128)(2,1)}, u32[]{:S(2)}, u32[]{:S(2)}) async-start(bf16[64,16,1792]{2,1,0:T(8,128)(2,1)} %bitcast.114), calls=%async_computation.4 | async-start | bytes 7340032 | tf_op jit(solution)/shard_map/all_to_all | solution.py:92
where the time goes:
time: 567 us; the launch traced here: 557 us
  waiting for transfers between devices  386 us (68%)
  starting transfers between devices  55.5 us (10%)
  matrix products  52.6 us (9%)
  other arithmetic  38.3 us (7%)
  local copies, waits for them, and re-layouts  24.1 us (4%)
    all_to_all x2, waiting for transfers between devices, local(): lax.all_to_all(rows_out.reshape(n_groups, send_cap, chunk), 'group', spli...  152 us
    ppermute x12, waiting for transfers between devices, shifted(): lax.ppermute(array, 'local', [(i, (i + shift) % n_local) for i in range(n...  140 us
    all_to_all x2, waiting for transfers between devices, local(): lax.all_to_all(group_part.reshape(n_groups, send_cap, chunk), 'group', sp...  86.4 us
    dot_general x8, matrix products, one_hot_dot(): jnp.einsum(spec, select, values, preferred_element_type=jnp.float32)  29.7 us
    ppermute x12, starting transfers between devices, shifted(): lax.ppermute(array, 'local', [(i, (i + shift) % n_local) for i in range(n...  16.3 us
    reduce_sum x2, other arithmetic, local(): jnp.sum(jnp.where(owner_c[:, :, None, None], stacked.astype(jnp.float32)[...  15.2 us
    all_to_all x2, starting transfers between devices, local(): lax.all_to_all(group_part.reshape(n_groups, send_cap, chunk), 'group', sp...  13.6 us
    all_to_all x1, starting transfers between devices, local(): lax.all_to_all(meta_out, 'group', split_axis=0, concat_axis=0, tiled=True)  13 us
  transfers between devices with their start and end apart: 17, of which 13 were waited for; matrix products, arithmetic and copies ran while one was open for 10% of the time, Pallas kernels for 0%

commit v1 on v0

--- a/solution.py
+++ b/solution.py
@@ -3,7 +3,7 @@
 from jax import lax
 from jax.sharding import PartitionSpec as P
 
-N_CHUNK = 2
+N_CHUNK = 4
 
 
 def shifted(array, shift):
@@ -38,19 +38,26 @@
     match_send = chosen[:, :, None] & (send_slot[:, :, None] == slot_line)
     source_row = jnp.sum(jnp.where(match_send, token_line[:, None, None], 0), axis=0)
     send_used = jnp.any(match_send, axis=0)
-    gates_out = jnp.where(send_used[:, :, None], gate_table[source_row, group_line[:, None]], 0.0)
-    flags_out = (send_used[:, :, None] & named[source_row, group_line[:, None]]).astype(jnp.float32)
-    meta_out = jnp.concatenate([gates_out, flags_out], axis=2)
-    meta_in = lax.all_to_all(meta_out, "group", split_axis=0, concat_axis=0, tiled=True)
-    meta_in = meta_in.reshape(arrived_count, 2 * per_group)
-    arrived_gates = meta_in[:, :per_group]
-    wanted = meta_in[:, per_group:] > 0.5
-    arrive_rank = jnp.cumsum(wanted.astype(jnp.int32), axis=0) - 1
-    taken = wanted & (arrive_rank < expert_cap)
-    cap_line = jnp.arange(expert_cap, dtype=jnp.int32)
-    match_expert = taken[:, :, None] & (arrive_rank[:, :, None] == cap_line)
-    expert_gates = jnp.sum(jnp.where(match_expert, arrived_gates[:, :, None], 0.0), axis=0)
-    pick = match_expert.reshape(arrived_count, per_group * expert_cap).astype(jnp.bfloat16)
+    gates_out = jnp.sum(jnp.where(match_send[:, :, :, None], gate_table[:, :, None, :], 0.0), axis=0)
+    flags_out = jnp.any(match_send[:, :, :, None] & named[:, :, None, :], axis=0).astype(jnp.bfloat16)
+    gates_hi = gates_out.astype(jnp.bfloat16)
+    gates_lo = (gates_out - gates_hi.astype(jnp.float32)).astype(jnp.bfloat16)
+    meta_out = jnp.concatenate([gates_hi, gates_lo, flags_out], axis=2)
+    meta_width = 128
+    meta_out = jnp.pad(meta_out, ((0, 0), (0, 0), (0, meta_width - 3 * per_group)))
+
+    def route(meta_in):
+        meta_in = meta_in.reshape(arrived_count, meta_width)[:, : 3 * per_group].astype(jnp.float32)
+        arrived_gates = meta_in[:, :per_group] + meta_in[:, per_group : 2 * per_group]
+        wanted = meta_in[:, 2 * per_group :] > 0.5
+        arrive_rank = jnp.cumsum(wanted.astype(jnp.int32), axis=0) - 1
+        taken = wanted & (arrive_rank < expert_cap)
+        cap_line = jnp.arange(expert_cap, dtype=jnp.int32)
+        match_expert = taken[:, :, None] & (arrive_rank[:, :, None] == cap_line)
+        expert_gates = jnp.sum(jnp.where(match_expert, arrived_gates[:, :, None], 0.0), axis=0)
+        pick = match_expert.reshape(arrived_count, per_group * expert_cap).astype(jnp.bfloat16)
+        return expert_gates, pick
+
     send_select = match_send.reshape(tok_rows, arrived_count).astype(jnp.bfloat16)
     here = lax.axis_index("local")
     device_line = jnp.arange(n_local, dtype=jnp.int32)
@@ -60,9 +67,13 @@
     for c in range(N_CHUNK):
         cols = slice(c * chunk, (c + 1) * chunk)
         rows_out = one_hot_dot(send_select, tokens[:, cols], "tk,td->kd")
-        rows_in = lax.all_to_all(
-            rows_out.reshape(n_groups, send_cap, chunk), "group", split_axis=0, concat_axis=0, tiled=True
-        ).reshape(arrived_count, chunk)
+        rows_out = rows_out.reshape(n_groups, send_cap, chunk)
+        if c == 0:
+            rows_out = jnp.concatenate([rows_out, meta_out], axis=2)
+        rows_in = lax.all_to_all(rows_out, "group", split_axis=0, concat_axis=0, tiled=True)
+        if c == 0:
+            expert_gates, pick = route(rows_in[:, :, chunk:])
+        rows_in = rows_in[:, :, :chunk].reshape(arrived_count, chunk)
         expert_rows = one_hot_dot(pick, rows_in, "ak,ad->kd").reshape(per_group, expert_cap, chunk)
         blocks = []
         for shift in range(n_local):

time: 567 us -> 568 us (level)
  starting transfers between devices: 55.5 us -> 102 us
  waiting for transfers between devices: 386 us -> 341 us
  matrix products: 52.6 us -> 67.7 us
  local copies, waits for them, and re-layouts: 24.1 us -> 13.9 us
  other arithmetic: 38.3 us -> 31.3 us
    all_to_all x2 -> x4, waiting for transfers between devices: 86.4 us -> 46.5 us  [local(): lax.all_to_all(group_part.reshape(n_groups, send_cap, chunk), 'group', sp...]
    all_to_all x2 -> x4, starting transfers between devices: 13.6 us -> 36.7 us  [local(): lax.all_to_all(group_part.reshape(n_groups, send_cap, chunk), 'group', sp...]
    ppermute x12 -> x24, starting transfers between devices: 16.3 us -> 32.3 us  [shifted(): lax.ppermute(array, 'local', [(i, (i + shift) % n_local) for i in range(n...]
    gather x4 -> x0, local copies, waits for them, and re-layouts: 13.1 us -> none  [the longest x2 7.08 us: local(): gate_table[source_row, group_line[:, None]]]
    all_to_all x3 -> x4, starting transfers between devices: 25.6 us -> 33.5 us  [local(): lax.all_to_all(rows_out, 'group', split_axis=0, concat_axis=0, tiled=True)]
    unnamed x16 -> x34, local copies, waits for them, and re-layouts: 0.92 us -> 7.97 us
    dot_general x2 -> x4, matrix products: 6.99 us -> 12.4 us  [local(): jnp.dot(hidden, w_down[:, cols], preferred_element_type=jnp.float32)]
    dot_general x8 -> x16, matrix products: 29.7 us -> 34.7 us  [one_hot_dot(): jnp.einsum(spec, select, values, preferred_element_type=jnp.float32)]
  transfers between devices with their start and end apart: 17 -> 32, of which waited for: 13 -> 23; matrix products, arithmetic and copies ran while one was open for 10% -> 14% of each run, Pallas kernels for 0% -> 0%
where the time goes in v1:
time: 568 us; the launch traced here: 557 us
  waiting for transfers between devices  341 us (60%)
  starting transfers between devices  102 us (18%)
  matrix products  67.7 us (12%)
  other arithmetic  31.3 us (6%)
  local copies, waits for them, and re-layouts  13.9 us (2%)
    all_to_all x4, waiting for transfers between devices, local(): lax.all_to_all(rows_out, 'group', split_axis=0, concat_axis=0, tiled=True)  158 us
    ppermute x24, waiting for transfers between devices, shifted(): lax.ppermute(array, 'local', [(i, (i + shift) % n_local) for i in range(n...  136 us
    all_to_all x4, waiting for transfers between devices, local(): lax.all_to_all(group_part.reshape(n_groups, send_cap, chunk), 'group', sp...  46.5 us
    all_to_all x4, starting transfers between devices, local(): lax.all_to_all(group_part.reshape(n_groups, send_cap, chunk), 'group', sp...  36.7 us
    dot_general x16, matrix products, one_hot_dot(): jnp.einsum(spec, select, values, preferred_element_type=jnp.float32)  34.7 us
    all_to_all x4, starting transfers between devices, local(): lax.all_to_all(rows_out, 'group', split_axis=0, concat_axis=0, tiled=True)  33.5 us
    ppermute x24, starting transfers between devices, shifted(): lax.ppermute(array, 'local', [(i, (i + shift) % n_local) for i in range(n...  32.3 us
    reduce_sum x4, other arithmetic, local(): jnp.sum(jnp.where(owner_c[:, :, None, None], stacked.astype(jnp.float32)[...  13.3 us
  transfers between devices with their start and end apart: 32, of which 23 were waited for; matrix products, arithmetic and copies ran while one was open for 14% of the time, Pallas kernels for 0%

profile of v1, /device:TPU:1, one launch (start us, length us, event | category | flops | bytes accessed | tf_op | source)
XLA Modules:
  0.0 557.4 jit_solution(9945042623235159901)
XLA Ops:
  1.8 2.8 convolution_convert_fusion.4
  4.6 13.1 %all-to-all-start.3 = ((bf16[64,16,896]{2,1,0:T(8,128)(2,1)}), bf16[64,16,896]{2,1,0:T(8,128)(2,1)S(1)}, u32[]{:S(2)}, u32[]{:S(2)}) async-start(bf16[64,16,896]{2,1,0:T(8,128)(2,1)} %bitcast.28), calls=%async_computation.3 | async-start | bytes 3670016 | tf_op jit(solution)/shard_map/all_to_all | solution.py:73
  19.5 42.6 %all-to-all-done.3 = bf16[64,16,896]{2,1,0:T(8,128)(2,1)S(1)} async-done(((bf16[64,16,896]{2,1,0:T(8,128)(2,1)}), bf16[64,16,896]{2,1,0:T(8,128)(2,1)S(1)}, u32[]{:S(2)}, u32[]{:S(2)}) %all-to-all-start.3) | async-done | bytes 1835040 | tf_op jit(solution)/shard_map/all_to_all | solution.py:73
  63.3 6.6 %all-to-all-start.2 = ((bf16[64,16,896]{2,1,0:T(8,128)(2,1)}), bf16[64,16,896]{2,1,0:T(8,128)(2,1)S(1)}, u32[]{:S(2)}, u32[]{:S(2)}) async-start(bf16[64,16,896]{2,1,0:T(8,128)(2,1)} %bitcast.21), calls=%async_computation.2 | async-start | bytes 3670016 | tf_op jit(solution)/shard_map/all_to_all | solution.py:73
  74.3 40.1 %all-to-all-done.2 = bf16[64,16,896]{2,1,0:T(8,128)(2,1)S(1)} async-done(((bf16[64,16,896]{2,1,0:T(8,128)(2,1)}), bf16[64,16,896]{2,1,0:T(8,128)(2,1)S(1)}, u32[]{:S(2)}, u32[]{:S(2)}) %all-to-all-start.2) | async-done | bytes 1835040 | tf_op jit(solution)/shard_map/all_to_all | solution.py:73
  115.7 6.6 %all-to-all-start = ((bf16[64,16,1024]{2,1,0:T(8,128)(2,1)}), bf16[64,16,1024]{2,1,0:T(8,128)(2,1)S(1)}, u32[]{:S(2)}, u32[]{:S(2)}) async-start(bf16[64,16,1024]{2,1,0:T(8,128)(2,1)} %fusion.12), calls=%async_computation | async-start | bytes 4194304 | tf_op jit(solution)/shard_map/all_to_all | solution.py:73
  124.2 47.9 %all-to-all-done = bf16[64,16,1024]{2,1,0:T(8,128)(2,1)S(1)} async-done(((bf16[64,16,1024]{2,1,0:T(8,128)(2,1)}), bf16[64,16,1024]{2,1,0:T(8,128)(2,1)S(1)}, u32[]{:S(2)}, u32[]{:S(2)}) %all-to-all-start) | async-done | bytes 2097184 | tf_op jit(solution)/shard_map/all_to_all | solution.py:73
  172.0 7.1 %all-to-all-start.1 = ((bf16[64,16,896]{2,1,0:T(8,128)(2,1)}), bf16[64,16,896]{2,1,0:T(8,128)(2,1)}, u32[]{:S(2)}, u32[]{:S(2)}) async-start(bf16[64,16,896]{2,1,0:T(8,128)(2,1)} %bitcast.167), calls=%async_computation.1 | async-start | bytes 3670016 | tf_op jit(solution)/shard_map/all_to_all | solution.py:73
  181.2 3.0 convolution_convert_fusion.12
  185.7 2.9 collective-permute-start.11
  195.9 27.7 %all-to-all-done.1 = bf16[64,16,896]{2,1,0:T(8,128)(2,1)} async-done(((bf16[64,16,896]{2,1,0:T(8,128)(2,1)}), bf16[64,16,896]{2,1,0:T(8,128)(2,1)}, u32[]{:S(2)}, u32[]{:S(2)}) %all-to-all-start.1) | async-done | bytes 1835040 | tf_op jit(solution)/shard_map/all_to_all | solution.py:73
  223.5 3.0 convolution_convert_fusion.14
  233.9 3.1 fusion.30
  237.0 2.9 fusion.21
  245.3 2.8 fusion.32
  248.1 2.7 fusion.23
  250.9 10.2 %collective-permute-done.5 = bf16[320,896]{1,0:T(8,128)(2,1)S(1)} collective-permute-done((bf16[320,896]{1,0:T(8,128)(2,1)S(1)}, bf16[320,896]{1,0:T(8,128)(2,1)S(1)}, u32[]{:S(2)}, u32[]{:S(2)}) %collective-permute-start.5) | collective-permute-done | bytes 573472 | tf_op jit(solution)/shard_map/ppermute | solution.py:11
  261.1 7.5 %collective-permute-done.3 = bf16[320,896]{1,0:T(8,128)(2,1)S(1)} collective-permute-done((bf16[320,896]{1,0:T(8,128)(2,1)S(1)}, bf16[320,896]{1,0:T(8,128)(2,1)S(1)}, u32[]{:S(2)}, u32[]{:S(2)}) %collective-permute-start.3) | collective-permute-done | bytes 573472 | tf_op jit(solution)/shard_map/ppermute | solution.py:11
  271.6 3.6 collective-permute-done.2
  275.2 6.5 %collective-permute-done.1 = bf16[320,896]{1,0:T(8,128)(2,1)S(1)} collective-permute-done((bf16[320,896]{1,0:T(8,128)(2,1)S(1)}, bf16[320,896]{1,0:T(8,128)(2,1)S(1)}, u32[]{:S(2)}, u32[]{:S(2)}) %collective-permute-start.1) | collective-permute-done | bytes 573472 | tf_op jit(solution)/shard_map/ppermute | solution.py:11
  281.7 11.4 %collective-permute-done = bf16[320,896]{1,0:T(8,128)(2,1)S(1)} collective-permute-done((bf16[320,896]{1,0:T(8,128)(2,1)S(1)}, bf16[320,896]{1,0:T(8,128)(2,1)S(1)}, u32[]{:S(2)}, u32[]{:S(2)}) %collective-permute-start) | collective-permute-done | bytes 573472 | tf_op jit(solution)/shard_map/ppermute | solution.py:11
  294.8 4.4 multiply_convert_fusion
  299.2 3.2 convolution_convert_fusion
  307.3 9.6 %collective-permute-done.23 = bf16[320,896]{1,0:T(8,128)(2,1)S(1)} collective-permute-done((bf16[320,896]{1,0:T(8,128)(2,1)S(1)}, bf16[320,896]{1,0:T(8,128)(2,1)S(1)}, u32[]{:S(2)}, u32[]{:S(2)}) %collective-permute-start.23) | collective-permute-done | bytes 573472 | tf_op jit(solution)/shard_map/ppermute | solution.py:11
  316.8 11.0 %collective-permute-done.22 = bf16[320,896]{1,0:T(8,128)(2,1)S(1)} collective-permute-done((bf16[320,896]{1,0:T(8,128)(2,1)S(1)}, bf16[320,896]{1,0:T(8,128)(2,1)S(1)}, u32[]{:S(2)}, u32[]{:S(2)}) %collective-permute-start.22) | collective-permute-done | bytes 573472 | tf_op jit(solution)/shard_map/ppermute | solution.py:11
  327.8 2.8 collective-permute-done.21
  333.4 3.3 select_reduce_fusion
  337.0 3.1 convolution_convert_fusion.8
  340.0 8.9 %all-to-all-start.7 = ((bf16[64,16,896]{2,1,0:T(8,128)(2,1)}), bf16[64,16,896]{2,1,0:T(8,128)(2,1)S(1)}, u32[]{:S(2)}, u32[]{:S(2)}) async-start(bf16[64,16,896]{2,1,0:T(8,128)(2,1)} %bitcast.177), calls=%async_computation.7 | async-start | bytes 3670016 | tf_op jit(solution)/shard_map/all_to_all | solution.py:103
  348.9 3.1 convolution_convert_fusion.1
  356.5 11.0 %collective-permute-done.20 = bf16[320,896]{1,0:T(8,128)(2,1)S(1)} collective-permute-done((bf16[320,896]{1,0:T(8,128)(2,1)S(1)}, bf16[320,896]{1,0:T(8,128)(2,1)S(1)}, u32[]{:S(2)}, u32[]{:S(2)}) %collective-permute-start.20) | collective-permute-done | bytes 573472 | tf_op jit(solution)/shard_map/ppermute | solution.py:11
  367.6 13.1 %collective-permute-done.19 = bf16[320,896]{1,0:T(8,128)(2,1)S(1)} collective-permute-done((bf16[320,896]{1,0:T(8,128)(2,1)S(1)}, bf16[320,896]{1,0:T(8,128)(2,1)S(1)}, u32[]{:S(2)}, u32[]{:S(2)}) %collective-permute-start.19) | collective-permute-done | bytes 573472 | tf_op jit(solution)/shard_map/ppermute | solution.py:11
  383.5 3.3 select_reduce_fusion.1
  388.2 3.1 convolution_convert_fusion.9
  393.3 9.3 %all-to-all-start.6 = ((bf16[64,16,896]{2,1,0:T(8,128)(2,1)}), bf16[64,16,896]{2,1,0:T(8,128)(2,1)}, u32[]{:S(2)}, u32[]{:S(2)}) async-start(bf16[64,16,896]{2,1,0:T(8,128)(2,1)} %bitcast.176), calls=%async_computation.6 | async-start | bytes 3670016 | tf_op jit(solution)/shard_map/all_to_all | solution.py:103
  402.6 3.1 convolution_convert_fusion.2
  409.8 11.5 %collective-permute-done.17 = bf16[320,896]{1,0:T(8,128)(2,1)S(1)} collective-permute-done((bf16[320,896]{1,0:T(8,128)(2,1)S(1)}, bf16[320,896]{1,0:T(8,128)(2,1)S(1)}, u32[]{:S(2)}, u32[]{:S(2)}) %collective-permute-start.17) | collective-permute-done | bytes 573472 | tf_op jit(solution)/shard_map/ppermute | solution.py:11
  421.3 12.8 %collective-permute-done.16 = bf16[320,896]{1,0:T(8,128)(2,1)S(1)} collective-permute-done((bf16[320,896]{1,0:T(8,128)(2,1)S(1)}, bf16[320,896]{1,0:T(8,128)(2,1)S(1)}, u32[]{:S(2)}, u32[]{:S(2)}) %collective-permute-start.16) | collective-permute-done | bytes 573472 | tf_op jit(solution)/shard_map/ppermute | solution.py:11
  436.9 3.3 select_reduce_fusion.2
  441.6 3.1 convolution_convert_fusion.10
  447.0 9.2 %all-to-all-start.5 = ((bf16[64,16,896]{2,1,0:T(8,128)(2,1)}), bf16[64,16,896]{2,1,0:T(8,128)(2,1)}, u32[]{:S(2)}, u32[]{:S(2)}) async-start(bf16[64,16,896]{2,1,0:T(8,128)(2,1)} %bitcast.175), calls=%async_computation.5 | async-start | bytes 3670016 | tf_op jit(solution)/shard_map/all_to_all | solution.py:103
  456.1 3.1 convolution_convert_fusion.3
  463.3 11.5 %collective-permute-done.14 = bf16[320,896]{1,0:T(8,128)(2,1)S(1)} collective-permute-done((bf16[320,896]{1,0:T(8,128)(2,1)S(1)}, bf16[320,896]{1,0:T(8,128)(2,1)S(1)}, u32[]{:S(2)}, u32[]{:S(2)}) %collective-permute-start.14) | collective-permute-done | bytes 573472 | tf_op jit(solution)/shard_map/ppermute | solution.py:11
  474.8 13.0 %collective-permute-done.13 = bf16[320,896]{1,0:T(8,128)(2,1)S(1)} collective-permute-done((bf16[320,896]{1,0:T(8,128)(2,1)S(1)}, bf16[320,896]{1,0:T(8,128)(2,1)S(1)}, u32[]{:S(2)}, u32[]{:S(2)}) %collective-permute-start.13) | collective-permute-done | bytes 573472 | tf_op jit(solution)/shard_map/ppermute | solution.py:11
  490.7 3.3 select_reduce_fusion.3
  495.3 3.1 convolution_convert_fusion.11
  500.5 9.4 %all-to-all-start.4 = ((bf16[64,16,896]{2,1,0:T(8,128)(2,1)}), bf16[64,16,896]{2,1,0:T(8,128)(2,1)}, u32[]{:S(2)}, u32[]{:S(2)}) async-start(bf16[64,16,896]{2,1,0:T(8,128)(2,1)} %bitcast.178), calls=%async_computation.4 | async-start | bytes 3670016 | tf_op jit(solution)/shard_map/all_to_all | solution.py:103
  514.2 40.0 %all-to-all-done.4 = bf16[64,16,896]{2,1,0:T(8,128)(2,1)} async-done(((bf16[64,16,896]{2,1,0:T(8,128)(2,1)}), bf16[64,16,896]{2,1,0:T(8,128)(2,1)}, u32[]{:S(2)}, u32[]{:S(2)}) %all-to-all-start.4) | async-done | bytes 1835040 | tf_op jit(solution)/shard_map/all_to_all | solution.py:103
  (148 shorter events, 86.5 us)
Async XLA Ops:
  4.6 13.1 %copy-start.9 = (bf16[64,3584]{1,0:T(8,128)(2,1)S(1)}, bf16[64,3584]{1,0:T(8,128)(2,1)}, u32[]{:S(2)}) copy-start(bf16[64,3584]{1,0:T(8,128)(2,1)} %param.6) | copy-start | bytes 1376260
  4.6 57.5 %all-to-all-start.3 = ((bf16[64,16,896]{2,1,0:T(8,128)(2,1)}), bf16[64,16,896]{2,1,0:T(8,128)(2,1)S(1)}, u32[]{:S(2)}, u32[]{:S(2)}) async-start(bf16[64,16,896]{2,1,0:T(8,128)(2,1)} %bitcast.28), calls=%async_computation.3 | async-start | bytes 3670016 | tf_op jit(solution)/shard_map/all_to_all | solution.py:73
  19.5 51.4 %copy-start.10 = (f32[64,8]{0,1:T(8,128)S(1)}, f32[64,8]{0,1:T(8,128)}, u32[]{:S(2)}) copy-start(f32[64,8]{0,1:T(8,128)} %param.8) | copy-start | bytes 6148
  62.1 1.2 copy-start.2
  63.3 51.1 %all-to-all-start.2 = ((bf16[64,16,896]{2,1,0:T(8,128)(2,1)}), bf16[64,16,896]{2,1,0:T(8,128)(2,1)S(1)}, u32[]{:S(2)}, u32[]{:S(2)}) async-start(bf16[64,16,896]{2,1,0:T(8,128)(2,1)} %bitcast.21), calls=%async_computation.2 | async-start | bytes 3670016 | tf_op jit(solution)/shard_map/all_to_all | solution.py:73
  114.4 1.3 copy-start
  115.7 56.4 %all-to-all-start = ((bf16[64,16,1024]{2,1,0:T(8,128)(2,1)}), bf16[64,16,1024]{2,1,0:T(8,128)(2,1)S(1)}, u32[]{:S(2)}, u32[]{:S(2)}) async-start(bf16[64,16,1024]{2,1,0:T(8,128)(2,1)} %fusion.12), calls=%async_computation | async-start | bytes 4194304 | tf_op jit(solution)/shard_map/all_to_all | solution.py:73
  172.0 51.5 %all-to-all-start.1 = ((bf16[64,16,896]{2,1,0:T(8,128)(2,1)}), bf16[64,16,896]{2,1,0:T(8,128)(2,1)}, u32[]{:S(2)}, u32[]{:S(2)}) async-start(bf16[64,16,896]{2,1,0:T(8,128)(2,1)} %bitcast.167), calls=%async_computation.1 | async-start | bytes 3670016 | tf_op jit(solution)/shard_map/all_to_all | solution.py:73
  184.2 5.4 copy-start.1
  185.7 43.0 %collective-permute-start.11 = (bf16[320,896]{1,0:T(8,128)(2,1)}, bf16[320,896]{1,0:T(8,128)(2,1)}, u32[]{:S(2)}, u32[]{:S(2)}) collective-permute-start(bf16[320,896]{1,0:T(8,128)(2,1)} %get-tuple-element.68), channel_id=1, source_target_pairs={{0,3},{1,0},{2,1},{3,2},{4,7},{5,4},{6,5},{7,6},{8,11},{9,8},{10,9... | collective-permute-start | bytes 1720328 | tf_op jit(solution)/shard_map/ppermute | solution.py:11
  188.6 42.2 %collective-permute-start.10 = (bf16[320,896]{1,0:T(8,128)(2,1)}, bf16[320,896]{1,0:T(8,128)(2,1)}, u32[]{:S(2)}, u32[]{:S(2)}) collective-permute-start(bf16[320,896]{1,0:T(8,128)(2,1)} %get-tuple-element.69), channel_id=1, source_target_pairs={{0,2},{1,3},{2,0},{3,1},{4,6},{5,7},{6,4},{7,5},{8,10},{9,11},{10,... | collective-permute-start | bytes 1720328 | tf_op jit(solution)/shard_map/ppermute | solution.py:11
  189.0 43.3 %collective-permute-start.9 = (bf16[320,896]{1,0:T(8,128)(2,1)}, bf16[320,896]{1,0:T(8,128)(2,1)}, u32[]{:S(2)}, u32[]{:S(2)}) collective-permute-start(bf16[320,896]{1,0:T(8,128)(2,1)} %get-tuple-element.70), channel_id=1, source_target_pairs={{0,1},{1,2},{2,3},{3,0},{4,5},{5,6},{6,7},{7,4},{8,9},{9,10},{10,1... | collective-permute-start | bytes 1720328 | tf_op jit(solution)/shard_map/ppermute | solution.py:11
  192.5 47.5 %collective-permute-start.8 = (bf16[320,896]{1,0:T(8,128)(2,1)}, bf16[320,896]{1,0:T(8,128)(2,1)}, u32[]{:S(2)}, u32[]{:S(2)}) collective-permute-start(bf16[320,896]{1,0:T(8,128)(2,1)} %get-tuple-element.64), channel_id=1, source_target_pairs={{0,3},{1,0},{2,1},{3,2},{4,7},{5,4},{6,5},{7,6},{8,11},{9,8},{10,9... | collective-permute-start | bytes 1720328 | tf_op jit(solution)/shard_map/ppermute | solution.py:11
  194.4 46.0 %collective-permute-start.7 = (bf16[320,896]{1,0:T(8,128)(2,1)}, bf16[320,896]{1,0:T(8,128)(2,1)}, u32[]{:S(2)}, u32[]{:S(2)}) collective-permute-start(bf16[320,896]{1,0:T(8,128)(2,1)} %get-tuple-element.65), channel_id=1, source_target_pairs={{0,2},{1,3},{2,0},{3,1},{4,6},{5,7},{6,4},{7,5},{8,10},{9,11},{10,... | collective-permute-start | bytes 1720328 | tf_op jit(solution)/shard_map/ppermute | solution.py:11
  226.9 7.0 %copy-start.11 = (bf16[3584,512]{1,0:T(8,128)(2,1)S(1)}, bf16[3584,512]{1,0:T(8,128)(2,1)}, u32[]{:S(2)}) copy-start(bf16[3584,512]{1,0:T(8,128)(2,1)} %param.9) | copy-start | bytes 11010052
  228.5 1.1 copy-start.7
  228.5 5.4 copy-start.8
  229.5 14.1 %collective-permute-start.6 = (bf16[320,896]{1,0:T(8,128)(2,1)S(1)}, bf16[320,896]{1,0:T(8,128)(2,1)S(1)}, u32[]{:S(2)}, u32[]{:S(2)}) collective-permute-start(bf16[320,896]{1,0:T(8,128)(2,1)S(1)} %copy-done.7), channel_id=1, source_target_pairs={{0,1},{1,2},{2,3},{3,0},{4,5},{5,6},{6,7},{7,4},{8,9},{9,10},{10,1... | collective-permute-start | bytes 1720328 | tf_op jit(solution)/shard_map/ppermute | solution.py:11
  230.8 30.2 %collective-permute-start.5 = (bf16[320,896]{1,0:T(8,128)(2,1)S(1)}, bf16[320,896]{1,0:T(8,128)(2,1)S(1)}, u32[]{:S(2)}, u32[]{:S(2)}) collective-permute-start(bf16[320,896]{1,0:T(8,128)(2,1)S(1)} %get-tuple-element.60), channel_id=1, source_target_pairs={{0,3},{1,0},{2,1},{3,2},{4,7},{5,4},{6,5},{7,6},{8,11},{9,8},{10,9... | collective-permute-start | bytes 1720328 | tf_op jit(solution)/shard_map/ppermute | solution.py:11
  232.3 28.8 %collective-permute-start.4 = (bf16[320,896]{1,0:T(8,128)(2,1)S(1)}, bf16[320,896]{1,0:T(8,128)(2,1)S(1)}, u32[]{:S(2)}, u32[]{:S(2)}) collective-permute-start(bf16[320,896]{1,0:T(8,128)(2,1)S(1)} %get-tuple-element.61), channel_id=1, source_target_pairs={{0,2},{1,3},{2,0},{3,1},{4,6},{5,7},{6,4},{7,5},{8,10},{9,11},{10,... | collective-permute-start | bytes 1720328 | tf_op jit(solution)/shard_map/ppermute | solution.py:11
  233.9 3.1 copy-start.12
  240.0 28.6 %collective-permute-start.3 = (bf16[320,896]{1,0:T(8,128)(2,1)S(1)}, bf16[320,896]{1,0:T(8,128)(2,1)S(1)}, u32[]{:S(2)}, u32[]{:S(2)}) collective-permute-start(bf16[320,896]{1,0:T(8,128)(2,1)S(1)} %get-tuple-element.62), channel_id=1, source_target_pairs={{0,1},{1,2},{2,3},{3,0},{4,5},{5,6},{6,7},{7,4},{8,9},{9,10},{10,1... | collective-permute-start | bytes 1720328 | tf_op jit(solution)/shard_map/ppermute | solution.py:11
  240.5 34.8 %collective-permute-start.2 = (bf16[320,896]{1,0:T(8,128)(2,1)S(1)}, bf16[320,896]{1,0:T(8,128)(2,1)S(1)}, u32[]{:S(2)}, u32[]{:S(2)}) collective-permute-start(bf16[320,896]{1,0:T(8,128)(2,1)S(1)} %get-tuple-element.56), channel_id=1, source_target_pairs={{0,3},{1,0},{2,1},{3,2},{4,7},{5,4},{6,5},{7,6},{8,11},{9,8},{10,9... | collective-permute-start | bytes 1720328 | tf_op jit(solution)/shard_map/ppermute | solution.py:11
  243.7 38.1 %collective-permute-start.1 = (bf16[320,896]{1,0:T(8,128)(2,1)S(1)}, bf16[320,896]{1,0:T(8,128)(2,1)S(1)}, u32[]{:S(2)}, u32[]{:S(2)}) collective-permute-start(bf16[320,896]{1,0:T(8,128)(2,1)S(1)} %get-tuple-element.57), channel_id=1, source_target_pairs={{0,2},{1,3},{2,0},{3,1},{4,6},{5,7},{6,4},{7,5},{8,10},{9,11},{10,... | collective-permute-start | bytes 1720328 | tf_op jit(solution)/shard_map/ppermute | solution.py:11
  261.1 32.1 %collective-permute-start = (bf16[320,896]{1,0:T(8,128)(2,1)S(1)}, bf16[320,896]{1,0:T(8,128)(2,1)S(1)}, u32[]{:S(2)}, u32[]{:S(2)}) collective-permute-start(bf16[320,896]{1,0:T(8,128)(2,1)S(1)} %get-tuple-element.58), channel_id=1, source_target_pairs={{0,1},{1,2},{2,3},{3,0},{4,5},{5,6},{6,7},{7,4},{8,9},{9,10},{10,1... | collective-permute-start | bytes 1720328 | tf_op jit(solution)/shard_map/ppermute | solution.py:11
  299.2 3.2 copy-start.13
  302.6 14.3 %collective-permute-start.23 = (bf16[320,896]{1,0:T(8,128)(2,1)S(1)}, bf16[320,896]{1,0:T(8,128)(2,1)S(1)}, u32[]{:S(2)}, u32[]{:S(2)}) collective-permute-start(bf16[320,896]{1,0:T(8,128)(2,1)S(1)} %get-tuple-element.52), channel_id=1, source_target_pairs={{0,1},{1,2},{2,3},{3,0},{4,5},{5,6},{6,7},{7,4},{8,9},{9,10},{10,1... | collective-permute-start | bytes 1720328 | tf_op jit(solution)/shard_map/ppermute | solution.py:11
  302.7 25.1 %collective-permute-start.22 = (bf16[320,896]{1,0:T(8,128)(2,1)S(1)}, bf16[320,896]{1,0:T(8,128)(2,1)S(1)}, u32[]{:S(2)}, u32[]{:S(2)}) collective-permute-start(bf16[320,896]{1,0:T(8,128)(2,1)S(1)} %get-tuple-element.53), channel_id=1, source_target_pairs={{0,2},{1,3},{2,0},{3,1},{4,6},{5,7},{6,4},{7,5},{8,10},{9,11},{10,... | collective-permute-start | bytes 1720328 | tf_op jit(solution)/shard_map/ppermute | solution.py:11
  305.0 25.6 %collective-permute-start.21 = (bf16[320,896]{1,0:T(8,128)(2,1)S(1)}, bf16[320,896]{1,0:T(8,128)(2,1)S(1)}, u32[]{:S(2)}, u32[]{:S(2)}) collective-permute-start(bf16[320,896]{1,0:T(8,128)(2,1)S(1)} %get-tuple-element.54), channel_id=1, source_target_pairs={{0,3},{1,0},{2,1},{3,2},{4,7},{5,4},{6,5},{7,6},{8,11},{9,8},{10,9... | collective-permute-start | bytes 1720328 | tf_op jit(solution)/shard_map/ppermute | solution.py:11
  306.6 30.3 %copy-start.3 = (bf16[1024,640]{0,1:T(8,128)(2,1)}, bf16[1024,640]{0,1:T(8,128)(2,1)S(1)}, u32[]{:S(2)}) copy-start(bf16[1024,640]{0,1:T(8,128)(2,1)S(1)} %fusion.7) | copy-start | bytes 3932164
  340.0 53.3 %all-to-all-start.7 = ((bf16[64,16,896]{2,1,0:T(8,128)(2,1)}), bf16[64,16,896]{2,1,0:T(8,128)(2,1)S(1)}, u32[]{:S(2)}, u32[]{:S(2)}) async-start(bf16[64,16,896]{2,1,0:T(8,128)(2,1)} %bitcast.177), calls=%async_computation.7 | async-start | bytes 3670016 | tf_op jit(solution)/shard_map/all_to_all | solution.py:103
  352.2 15.4 %collective-permute-start.20 = (bf16[320,896]{1,0:T(8,128)(2,1)S(1)}, bf16[320,896]{1,0:T(8,128)(2,1)S(1)}, u32[]{:S(2)}, u32[]{:S(2)}) collective-permute-start(bf16[320,896]{1,0:T(8,128)(2,1)S(1)} %get-tuple-element.48), channel_id=1, source_target_pairs={{0,1},{1,2},{2,3},{3,0},{4,5},{5,6},{6,7},{7,4},{8,9},{9,10},{10,1... | collective-permute-start | bytes 1720328 | tf_op jit(solution)/shard_map/ppermute | solution.py:11
  353.6 27.1 %collective-permute-start.19 = (bf16[320,896]{1,0:T(8,128)(2,1)S(1)}, bf16[320,896]{1,0:T(8,128)(2,1)S(1)}, u32[]{:S(2)}, u32[]{:S(2)}) collective-permute-start(bf16[320,896]{1,0:T(8,128)(2,1)S(1)} %get-tuple-element.49), channel_id=1, source_target_pairs={{0,2},{1,3},{2,0},{3,1},{4,6},{5,7},{6,4},{7,5},{8,10},{9,11},{10,... | collective-permute-start | bytes 1720328 | tf_op jit(solution)/shard_map/ppermute | solution.py:11
  355.8 24.9 %collective-permute-start.18 = (bf16[320,896]{1,0:T(8,128)(2,1)S(1)}, bf16[320,896]{1,0:T(8,128)(2,1)S(1)}, u32[]{:S(2)}, u32[]{:S(2)}) collective-permute-start(bf16[320,896]{1,0:T(8,128)(2,1)S(1)} %get-tuple-element.50), channel_id=1, source_target_pairs={{0,3},{1,0},{2,1},{3,2},{4,7},{5,4},{6,5},{7,6},{8,11},{9,8},{10,9... | collective-permute-start | bytes 1720328 | tf_op jit(solution)/shard_map/ppermute | solution.py:11
  386.9 1.3 copy-start.4
  393.3 53.6 %all-to-all-start.6 = ((bf16[64,16,896]{2,1,0:T(8,128)(2,1)}), bf16[64,16,896]{2,1,0:T(8,128)(2,1)}, u32[]{:S(2)}, u32[]{:S(2)}) async-start(bf16[64,16,896]{2,1,0:T(8,128)(2,1)} %bitcast.176), calls=%async_computation.6 | async-start | bytes 3670016 | tf_op jit(solution)/shard_map/all_to_all | solution.py:103
  405.9 15.4 %collective-permute-start.17 = (bf16[320,896]{1,0:T(8,128)(2,1)S(1)}, bf16[320,896]{1,0:T(8,128)(2,1)S(1)}, u32[]{:S(2)}, u32[]{:S(2)}) collective-permute-start(bf16[320,896]{1,0:T(8,128)(2,1)S(1)} %get-tuple-element.44), channel_id=1, source_target_pairs={{0,1},{1,2},{2,3},{3,0},{4,5},{5,6},{6,7},{7,4},{8,9},{9,10},{10,1... | collective-permute-start | bytes 1720328 | tf_op jit(solution)/shard_map/ppermute | solution.py:11
  407.1 27.0 %collective-permute-start.16 = (bf16[320,896]{1,0:T(8,128)(2,1)S(1)}, bf16[320,896]{1,0:T(8,128)(2,1)S(1)}, u32[]{:S(2)}, u32[]{:S(2)}) collective-permute-start(bf16[320,896]{1,0:T(8,128)(2,1)S(1)} %get-tuple-element.45), channel_id=1, source_target_pairs={{0,2},{1,3},{2,0},{3,1},{4,6},{5,7},{6,4},{7,5},{8,10},{9,11},{10,... | collective-permute-start | bytes 1720328 | tf_op jit(solution)/shard_map/ppermute | solution.py:11
  409.3 24.8 %collective-permute-start.15 = (bf16[320,896]{1,0:T(8,128)(2,1)S(1)}, bf16[320,896]{1,0:T(8,128)(2,1)S(1)}, u32[]{:S(2)}, u32[]{:S(2)}) collective-permute-start(bf16[320,896]{1,0:T(8,128)(2,1)S(1)} %get-tuple-element.46), channel_id=1, source_target_pairs={{0,3},{1,0},{2,1},{3,2},{4,7},{5,4},{6,5},{7,6},{8,11},{9,8},{10,9... | collective-permute-start | bytes 1720328 | tf_op jit(solution)/shard_map/ppermute | solution.py:11
  440.3 1.3 copy-start.5
  447.0 53.5 %all-to-all-start.5 = ((bf16[64,16,896]{2,1,0:T(8,128)(2,1)}), bf16[64,16,896]{2,1,0:T(8,128)(2,1)}, u32[]{:S(2)}, u32[]{:S(2)}) async-start(bf16[64,16,896]{2,1,0:T(8,128)(2,1)} %bitcast.175), calls=%async_computation.5 | async-start | bytes 3670016 | tf_op jit(solution)/shard_map/all_to_all | solution.py:103
  459.4 15.4 %collective-permute-start.14 = (bf16[320,896]{1,0:T(8,128)(2,1)S(1)}, bf16[320,896]{1,0:T(8,128)(2,1)S(1)}, u32[]{:S(2)}, u32[]{:S(2)}) collective-permute-start(bf16[320,896]{1,0:T(8,128)(2,1)S(1)} %get-tuple-element.40), channel_id=1, source_target_pairs={{0,1},{1,2},{2,3},{3,0},{4,5},{5,6},{6,7},{7,4},{8,9},{9,10},{10,1... | collective-permute-start | bytes 1720328 | tf_op jit(solution)/shard_map/ppermute | solution.py:11
  460.6 27.2 %collective-permute-start.13 = (bf16[320,896]{1,0:T(8,128)(2,1)S(1)}, bf16[320,896]{1,0:T(8,128)(2,1)S(1)}, u32[]{:S(2)}, u32[]{:S(2)}) collective-permute-start(bf16[320,896]{1,0:T(8,128)(2,1)S(1)} %get-tuple-element.41), channel_id=1, source_target_pairs={{0,2},{1,3},{2,0},{3,1},{4,6},{5,7},{6,4},{7,5},{8,10},{9,11},{10,... | collective-permute-start | bytes 1720328 | tf_op jit(solution)/shard_map/ppermute | solution.py:11
  463.0 24.8 %collective-permute-start.12 = (bf16[320,896]{1,0:T(8,128)(2,1)S(1)}, bf16[320,896]{1,0:T(8,128)(2,1)S(1)}, u32[]{:S(2)}, u32[]{:S(2)}) collective-permute-start(bf16[320,896]{1,0:T(8,128)(2,1)S(1)} %get-tuple-element.42), channel_id=1, source_target_pairs={{0,3},{1,0},{2,1},{3,2},{4,7},{5,4},{6,5},{7,6},{8,11},{9,8},{10,9... | collective-permute-start | bytes 1720328 | tf_op jit(solution)/shard_map/ppermute | solution.py:11
  494.0 1.3 copy-start.6
  500.5 53.7 %all-to-all-start.4 = ((bf16[64,16,896]{2,1,0:T(8,128)(2,1)}), bf16[64,16,896]{2,1,0:T(8,128)(2,1)}, u32[]{:S(2)}, u32[]{:S(2)}) async-start(bf16[64,16,896]{2,1,0:T(8,128)(2,1)} %bitcast.178), calls=%async_computation.4 | async-start | bytes 3670016 | tf_op jit(solution)/shard_map/all_to_all | solution.py:103

commit v2 on v1

--- a/solution.py
+++ b/solution.py
@@ -3,7 +3,16 @@
 from jax import lax
 from jax.sharding import PartitionSpec as P
 
-N_CHUNK = 4
+GO_UNITS = (10, 8, 6, 4)
+RET_UNITS = (4, 6, 8, 10)
+
+
+def bounds(units, width):
+    step = width // sum(units)
+    edges = [0]
+    for unit in units:
+        edges.append(edges[-1] + unit * step)
+    return [slice(a, b) for a, b in zip(edges[:-1], edges[1:])]
 
 
 def shifted(array, shift):
@@ -20,7 +29,6 @@
     n_local = lax.axis_size("local")
     per_group = n_local // 2
     tok_rows, width = tokens.shape
-    chunk = width // N_CHUNK
     send_cap = tok_rows // 4
     expert_cap = n_groups * send_cap * 5 // 16
     expert_count = n_groups * per_group
@@ -64,8 +72,8 @@
 
     gate_acc = None
     up_acc = None
-    for c in range(N_CHUNK):
-        cols = slice(c * chunk, (c + 1) * chunk)
+    for c, cols in enumerate(bounds(GO_UNITS, width)):
+        chunk = cols.stop - cols.start
         rows_out = one_hot_dot(send_select, tokens[:, cols], "tk,td->kd")
         rows_out = rows_out.reshape(n_groups, send_cap, chunk)
         if c == 0:
@@ -89,8 +97,8 @@
 
     outs = []
     owner = ((here + device_line) % n_local) // 2 == jnp.arange(per_group, dtype=jnp.int32)[:, None]
-    for c in range(N_CHUNK):
-        cols = slice(c * chunk, (c + 1) * chunk)
+    for cols in bounds(RET_UNITS, width):
+        chunk = cols.stop - cols.start
         partial_value = jnp.dot(hidden, w_down[:, cols], preferred_element_type=jnp.float32)
         partial_value = partial_value.astype(jnp.bfloat16).reshape(n_local, expert_cap, chunk)
         by_shift = [partial_value[0]] + [

time: 568 us -> 596 us (1.049)
  waiting for transfers between devices: 341 us -> 368 us
  matrix products: 67.7 us -> 60.4 us
    ppermute x24, waiting for transfers between devices: 136 us -> 153 us  [shifted(): lax.ppermute(array, 'local', [(i, (i + shift) % n_local) for i in range(n...]
    all_to_all x4, waiting for transfers between devices: 46.5 us -> 56.8 us  [local(): lax.all_to_all(group_part.reshape(n_groups, send_cap, chunk), 'group', sp...]
    all_to_all x4, starting transfers between devices: 36.7 us -> 42.8 us  [local(): lax.all_to_all(group_part.reshape(n_groups, send_cap, chunk), 'group', sp...]
    unnamed x34 -> x52, local copies, waits for them, and re-layouts: 7.97 us -> 12.9 us
  transfers between devices with their start and end apart: 32 -> 32, of which waited for: 23 -> 20; matrix products, arithmetic and copies ran while one was open for 14% -> 14% of each run, Pallas kernels for 0% -> 0%
where the time goes in v2:
time: 596 us; the launch traced here: 585 us
  waiting for transfers between devices  368 us (62%)
  starting transfers between devices  107 us (18%)
  matrix products  60.4 us (10%)
  other arithmetic  29.7 us (5%)
  local copies, waits for them, and re-layouts  18.6 us (3%)
    all_to_all x4, waiting for transfers between devices, local(): lax.all_to_all(rows_out, 'group', split_axis=0, concat_axis=0, tiled=True)  159 us
    ppermute x24, waiting for transfers between devices, shifted(): lax.ppermute(array, 'local', [(i, (i + shift) % n_local) for i in range(n...  153 us
    all_to_all x4, waiting for transfers between devices, local(): lax.all_to_all(group_part.reshape(n_groups, send_cap, chunk), 'group', sp...  56.8 us
    all_to_all x4, starting transfers between devices, local(): lax.all_to_all(group_part.reshape(n_groups, send_cap, chunk), 'group', sp...  42.8 us
    dot_general x16, matrix products, one_hot_dot(): jnp.einsum(spec, select, values, preferred_element_type=jnp.float32)  32.8 us
    all_to_all x4, starting transfers between devices, local(): lax.all_to_all(rows_out, 'group', split_axis=0, concat_axis=0, tiled=True)  32.8 us
    ppermute x24, starting transfers between devices, shifted(): lax.ppermute(array, 'local', [(i, (i + shift) % n_local) for i in range(n...  31.5 us
    unnamed x52, local copies, waits for them, and re-layouts  12.9 us
  transfers between devices with their start and end apart: 32, of which 20 were waited for; matrix products, arithmetic and copies ran while one was open for 14% of the time, Pallas kernels for 0%

profile of v2, /device:TPU:1, one launch (start us, length us, event | category | flops | bytes accessed | tf_op | source)
XLA Modules:
  0.0 585.0 jit_solution(17844235620897047117)
XLA Ops:
  4.1 13.0 %all-to-all-start.3 = ((bf16[64,16,512]{2,1,0:T(8,128)(2,1)}), bf16[64,16,512]{2,1,0:T(8,128)(2,1)S(1)}, u32[]{:S(2)}, u32[]{:S(2)}) async-start(bf16[64,16,512]{2,1,0:T(8,128)(2,1)} %bitcast.28), calls=%async_computation.3 | async-start | bytes 2097152 | tf_op jit(solution)/shard_map/all_to_all | solution.py:81
  18.8 26.4 %all-to-all-done.3 = bf16[64,16,512]{2,1,0:T(8,128)(2,1)S(1)} async-done(((bf16[64,16,512]{2,1,0:T(8,128)(2,1)}), bf16[64,16,512]{2,1,0:T(8,128)(2,1)S(1)}, u32[]{:S(2)}, u32[]{:S(2)}) %all-to-all-start.3) | async-done | bytes 1048608 | tf_op jit(solution)/shard_map/all_to_all | solution.py:81
  46.2 6.3 %all-to-all-start.2 = ((bf16[64,16,768]{2,1,0:T(8,128)(2,1)}), bf16[64,16,768]{2,1,0:T(8,128)(2,1)S(1)}, u32[]{:S(2)}, u32[]{:S(2)}) async-start(bf16[64,16,768]{2,1,0:T(8,128)(2,1)} %bitcast.21), calls=%async_computation.2 | async-start | bytes 3145728 | tf_op jit(solution)/shard_map/all_to_all | solution.py:81
  57.1 34.4 %all-to-all-done.2 = bf16[64,16,768]{2,1,0:T(8,128)(2,1)S(1)} async-done(((bf16[64,16,768]{2,1,0:T(8,128)(2,1)}), bf16[64,16,768]{2,1,0:T(8,128)(2,1)S(1)}, u32[]{:S(2)}, u32[]{:S(2)}) %all-to-all-start.2) | async-done | bytes 1572896 | tf_op jit(solution)/shard_map/all_to_all | solution.py:81
  92.8 6.4 %all-to-all-start = ((bf16[64,16,1408]{2,1,0:T(8,128)(2,1)}), bf16[64,16,1408]{2,1,0:T(8,128)(2,1)S(1)}, u32[]{:S(2)}, u32[]{:S(2)}) async-start(bf16[64,16,1408]{2,1,0:T(8,128)(2,1)} %fusion.6), calls=%async_computation | async-start | bytes 5767168 | tf_op jit(solution)/shard_map/all_to_all | solution.py:81
  99.1 3.0 convolution_convert_fusion.7
  102.1 63.6 %all-to-all-done = bf16[64,16,1408]{2,1,0:T(8,128)(2,1)S(1)} async-done(((bf16[64,16,1408]{2,1,0:T(8,128)(2,1)}), bf16[64,16,1408]{2,1,0:T(8,128)(2,1)S(1)}, u32[]{:S(2)}, u32[]{:S(2)}) %all-to-all-start) | async-done | bytes 2883616 | tf_op jit(solution)/shard_map/all_to_all | solution.py:81
  165.7 7.2 %all-to-all-start.1 = ((bf16[64,16,1024]{2,1,0:T(8,128)(2,1)}), bf16[64,16,1024]{2,1,0:T(8,128)(2,1)}, u32[]{:S(2)}, u32[]{:S(2)}) async-start(bf16[64,16,1024]{2,1,0:T(8,128)(2,1)} %bitcast.168), calls=%async_computation.1 | async-start | bytes 4194304 | tf_op jit(solution)/shard_map/all_to_all | solution.py:81
  174.9 2.3 convolution_convert_fusion.15
  178.3 2.7 collective-permute-start.11
  188.3 34.1 %all-to-all-done.1 = bf16[64,16,1024]{2,1,0:T(8,128)(2,1)} async-done(((bf16[64,16,1024]{2,1,0:T(8,128)(2,1)}), bf16[64,16,1024]{2,1,0:T(8,128)(2,1)}, u32[]{:S(2)}, u32[]{:S(2)}) %all-to-all-start.1) | async-done | bytes 2097184 | tf_op jit(solution)/shard_map/all_to_all | solution.py:81
  222.5 3.3 convolution_convert_fusion.11
  245.7 2.4 fusion.30
  248.1 2.4 fusion.28
  250.8 8.0 %collective-permute-done.4 = bf16[320,1024]{1,0:T(8,128)(2,1)S(1)} collective-permute-done((bf16[320,1024]{1,0:T(8,128)(2,1)S(1)}, bf16[320,1024]{1,0:T(8,128)(2,1)S(1)}, u32[]{:S(2)}, u32[]{:S(2)}) %collective-permute-start.4) | collective-permute-done | bytes 655392 | tf_op jit(solution)/shard_map/ppermute | solution.py:20
  258.8 13.7 %collective-permute-done.3 = bf16[320,1024]{1,0:T(8,128)(2,1)S(1)} collective-permute-done((bf16[320,1024]{1,0:T(8,128)(2,1)S(1)}, bf16[320,1024]{1,0:T(8,128)(2,1)S(1)}, u32[]{:S(2)}, u32[]{:S(2)}) %collective-permute-start.3) | collective-permute-done | bytes 655392 | tf_op jit(solution)/shard_map/ppermute | solution.py:20
  275.6 2.9 collective-permute-done.2
  278.5 12.0 %collective-permute-done.1 = bf16[320,1280]{1,0:T(8,128)(2,1)S(1)} collective-permute-done((bf16[320,1280]{1,0:T(8,128)(2,1)S(1)}, bf16[320,1280]{1,0:T(8,128)(2,1)S(1)}, u32[]{:S(2)}, u32[]{:S(2)}) %collective-permute-start.1) | collective-permute-done | bytes 819232 | tf_op jit(solution)/shard_map/ppermute | solution.py:20
  290.5 17.1 %collective-permute-done = bf16[320,1280]{1,0:T(8,128)(2,1)S(1)} collective-permute-done((bf16[320,1280]{1,0:T(8,128)(2,1)S(1)}, bf16[320,1280]{1,0:T(8,128)(2,1)S(1)}, u32[]{:S(2)}, u32[]{:S(2)}) %collective-permute-start) | collective-permute-done | bytes 819232 | tf_op jit(solution)/shard_map/ppermute | solution.py:20
  309.8 2.6 multiply_convert_fusion
  318.5 6.3 %collective-permute-done.14 = bf16[320,512]{1,0:T(8,128)(2,1)S(1)} collective-permute-done((bf16[320,512]{1,0:T(8,128)(2,1)S(1)}, bf16[320,512]{1,0:T(8,128)(2,1)S(1)}, u32[]{:S(2)}, u32[]{:S(2)}) %collective-permute-start.14) | collective-permute-done | bytes 327712 | tf_op jit(solution)/shard_map/ppermute | solution.py:20
  324.8 3.8 collective-permute-done.13
  328.6 3.6 collective-permute-done.12
  336.2 9.1 %all-to-all-start.4 = ((bf16[64,16,512]{2,1,0:T(8,128)(2,1)}), bf16[64,16,512]{2,1,0:T(8,128)(2,1)S(1)}, u32[]{:S(2)}, u32[]{:S(2)}) async-start(bf16[64,16,512]{2,1,0:T(8,128)(2,1)} %bitcast.42), calls=%async_computation.4 | async-start | bytes 2097152 | tf_op jit(solution)/shard_map/all_to_all | solution.py:111
  345.3 2.3 convolution_convert_fusion.4
  348.9 2.5 collective-permute-start.16
  351.6 9.8 %collective-permute-done.17 = bf16[320,768]{1,0:T(8,128)(2,1)S(1)} collective-permute-done((bf16[320,768]{1,0:T(8,128)(2,1)S(1)}, bf16[320,768]{1,0:T(8,128)(2,1)S(1)}, u32[]{:S(2)}, u32[]{:S(2)}) %collective-permute-start.17) | collective-permute-done | bytes 491552 | tf_op jit(solution)/shard_map/ppermute | solution.py:20
  361.4 11.4 %collective-permute-done.16 = bf16[320,768]{1,0:T(8,128)(2,1)S(1)} collective-permute-done((bf16[320,768]{1,0:T(8,128)(2,1)S(1)}, bf16[320,768]{1,0:T(8,128)(2,1)S(1)}, u32[]{:S(2)}, u32[]{:S(2)}) %collective-permute-start.16) | collective-permute-done | bytes 491552 | tf_op jit(solution)/shard_map/ppermute | solution.py:20
  375.3 3.0 select_reduce_fusion.2
  379.6 2.6 convolution_convert_fusion.9
  383.3 11.2 %all-to-all-start.5 = ((bf16[64,16,768]{2,1,0:T(8,128)(2,1)}), bf16[64,16,768]{2,1,0:T(8,128)(2,1)S(1)}, u32[]{:S(2)}, u32[]{:S(2)}) async-start(bf16[64,16,768]{2,1,0:T(8,128)(2,1)} %bitcast.177), calls=%async_computation.5 | async-start | bytes 3145728 | tf_op jit(solution)/shard_map/all_to_all | solution.py:111
  394.5 2.8 convolution_convert_fusion.2
  398.6 2.5 collective-permute-start.19
  401.3 13.6 %collective-permute-done.20 = bf16[320,1024]{1,0:T(8,128)(2,1)S(1)} collective-permute-done((bf16[320,1024]{1,0:T(8,128)(2,1)S(1)}, bf16[320,1024]{1,0:T(8,128)(2,1)S(1)}, u32[]{:S(2)}, u32[]{:S(2)}) %collective-permute-start.20) | collective-permute-done | bytes 655392 | tf_op jit(solution)/shard_map/ppermute | solution.py:20
  414.9 14.7 %collective-permute-done.19 = bf16[320,1024]{1,0:T(8,128)(2,1)S(1)} collective-permute-done((bf16[320,1024]{1,0:T(8,128)(2,1)S(1)}, bf16[320,1024]{1,0:T(8,128)(2,1)S(1)}, u32[]{:S(2)}, u32[]{:S(2)}) %collective-permute-start.19) | collective-permute-done | bytes 655392 | tf_op jit(solution)/shard_map/ppermute | solution.py:20
  429.9 3.0 convert_element_type.147
  432.9 3.6 select_reduce_fusion.1
  437.9 3.2 convolution_convert_fusion.8
  442.3 11.2 %all-to-all-start.6 = ((bf16[64,16,1024]{2,1,0:T(8,128)(2,1)}), bf16[64,16,1024]{2,1,0:T(8,128)(2,1)S(1)}, u32[]{:S(2)}, u32[]{:S(2)}) async-start(bf16[64,16,1024]{2,1,0:T(8,128)(2,1)} %bitcast.175), calls=%async_computation.6 | async-start | bytes 4194304 | tf_op jit(solution)/shard_map/all_to_all | solution.py:111
  453.5 3.6 convolution_convert_fusion
  458.2 2.8 collective-permute-start.22
  461.2 16.8 %collective-permute-done.23 = bf16[320,1280]{1,0:T(8,128)(2,1)S(1)} collective-permute-done((bf16[320,1280]{1,0:T(8,128)(2,1)S(1)}, bf16[320,1280]{1,0:T(8,128)(2,1)S(1)}, u32[]{:S(2)}, u32[]{:S(2)}) %collective-permute-start.23) | collective-permute-done | bytes 819232 | tf_op jit(solution)/shard_map/ppermute | solution.py:20
  478.0 18.4 %collective-permute-done.22 = bf16[320,1280]{1,0:T(8,128)(2,1)S(1)} collective-permute-done((bf16[320,1280]{1,0:T(8,128)(2,1)S(1)}, bf16[320,1280]{1,0:T(8,128)(2,1)S(1)}, u32[]{:S(2)}, u32[]{:S(2)}) %collective-permute-start.22) | collective-permute-done | bytes 819232 | tf_op jit(solution)/shard_map/ppermute | solution.py:20
  496.8 3.3 convert_element_type.152
  500.2 4.3 select_reduce_fusion
  505.9 3.8 convolution_convert_fusion.1
  511.0 11.2 %all-to-all-start.7 = ((bf16[64,16,1280]{2,1,0:T(8,128)(2,1)}), bf16[64,16,1280]{2,1,0:T(8,128)(2,1)S(1)}, u32[]{:S(2)}, u32[]{:S(2)}) async-start(bf16[64,16,1280]{2,1,0:T(8,128)(2,1)} %bitcast.172), calls=%async_computation.7 | async-start | bytes 5242880 | tf_op jit(solution)/shard_map/all_to_all | solution.py:111
  526.4 56.8 %all-to-all-done.7 = bf16[64,16,1280]{2,1,0:T(8,128)(2,1)S(1)} async-done(((bf16[64,16,1280]{2,1,0:T(8,128)(2,1)}), bf16[64,16,1280]{2,1,0:T(8,128)(2,1)S(1)}, u32[]{:S(2)}, u32[]{:S(2)}) %all-to-all-start.7) | async-done | bytes 2621472 | tf_op jit(solution)/shard_map/all_to_all | solution.py:111
  (166 shorter events, 78.7 us)
Async XLA Ops:
  0.0 17.1 %copy-start.15 = (bf16[64,3584]{1,0:T(8,128)(2,1)S(1)}, bf16[64,3584]{1,0:T(8,128)(2,1)}, u32[]{:S(2)}) copy-start(bf16[64,3584]{1,0:T(8,128)(2,1)} %param.6) | copy-start | bytes 1376260
  4.1 41.1 %all-to-all-start.3 = ((bf16[64,16,512]{2,1,0:T(8,128)(2,1)}), bf16[64,16,512]{2,1,0:T(8,128)(2,1)S(1)}, u32[]{:S(2)}, u32[]{:S(2)}) async-start(bf16[64,16,512]{2,1,0:T(8,128)(2,1)} %bitcast.28), calls=%async_computation.3 | async-start | bytes 2097152 | tf_op jit(solution)/shard_map/all_to_all | solution.py:81
  17.1 36.4 %copy-start.17 = (f32[64,8]{0,1:T(8,128)S(1)}, f32[64,8]{0,1:T(8,128)}, u32[]{:S(2)}) copy-start(f32[64,8]{0,1:T(8,128)} %param.8) | copy-start | bytes 6148
  46.2 45.3 %all-to-all-start.2 = ((bf16[64,16,768]{2,1,0:T(8,128)(2,1)}), bf16[64,16,768]{2,1,0:T(8,128)(2,1)S(1)}, u32[]{:S(2)}, u32[]{:S(2)}) async-start(bf16[64,16,768]{2,1,0:T(8,128)(2,1)} %bitcast.21), calls=%async_computation.2 | async-start | bytes 3145728 | tf_op jit(solution)/shard_map/all_to_all | solution.py:81
  92.8 72.9 %all-to-all-start = ((bf16[64,16,1408]{2,1,0:T(8,128)(2,1)}), bf16[64,16,1408]{2,1,0:T(8,128)(2,1)S(1)}, u32[]{:S(2)}, u32[]{:S(2)}) async-start(bf16[64,16,1408]{2,1,0:T(8,128)(2,1)} %fusion.6), calls=%async_computation | async-start | bytes 5767168 | tf_op jit(solution)/shard_map/all_to_all | solution.py:81
  165.7 56.8 %all-to-all-start.1 = ((bf16[64,16,1024]{2,1,0:T(8,128)(2,1)}), bf16[64,16,1024]{2,1,0:T(8,128)(2,1)}, u32[]{:S(2)}, u32[]{:S(2)}) async-start(bf16[64,16,1024]{2,1,0:T(8,128)(2,1)} %bitcast.168), calls=%async_computation.1 | async-start | bytes 4194304 | tf_op jit(solution)/shard_map/all_to_all | solution.py:81
  174.9 7.4 %copy-start.11 = (pred[1024,2,320]{0,2,1:T(32,128)(4,1)}, pred[1024,2,320]{0,2,1:T(32,128)(4,1)S(1)}, u32[]{:S(2)}) copy-start(pred[1024,2,320]{0,2,1:T(32,128)(4,1)S(1)} %fusion.8) | copy-start | bytes 1966084
  174.9 7.4 %copy-start.5 = (bf16[64,16,768]{2,1,0:T(8,128)(2,1)S(1)}, bf16[64,16,768]{2,1,0:T(8,128)(2,1)}, u32[]{:S(2)}) copy-start(bf16[64,16,768]{2,1,0:T(8,128)(2,1)} %copy-done.4) | copy-start | bytes 4718596
  178.3 52.5 %collective-permute-start.11 = (bf16[320,512]{1,0:T(8,128)(2,1)}, bf16[320,512]{1,0:T(8,128)(2,1)}, u32[]{:S(2)}, u32[]{:S(2)}) collective-permute-start(bf16[320,512]{1,0:T(8,128)(2,1)} %get-tuple-element.68), channel_id=1, source_target_pairs={{0,3},{1,0},{2,1},{3,2},{4,7},{5,4},{6,5},{7,6},{8,11},{9,8},{10,9... | collective-permute-start | bytes 983048 | tf_op jit(solution)/shard_map/ppermute | solution.py:20
  181.1 51.8 %collective-permute-start.10 = (bf16[320,512]{1,0:T(8,128)(2,1)}, bf16[320,512]{1,0:T(8,128)(2,1)}, u32[]{:S(2)}, u32[]{:S(2)}) collective-permute-start(bf16[320,512]{1,0:T(8,128)(2,1)} %get-tuple-element.69), channel_id=1, source_target_pairs={{0,2},{1,3},{2,0},{3,1},{4,6},{5,7},{6,4},{7,5},{8,10},{9,11},{10,... | collective-permute-start | bytes 983048 | tf_op jit(solution)/shard_map/ppermute | solution.py:20
  181.4 52.9 %collective-permute-start.9 = (bf16[320,512]{1,0:T(8,128)(2,1)}, bf16[320,512]{1,0:T(8,128)(2,1)}, u32[]{:S(2)}, u32[]{:S(2)}) collective-permute-start(bf16[320,512]{1,0:T(8,128)(2,1)} %get-tuple-element.70), channel_id=1, source_target_pairs={{0,1},{1,2},{2,3},{3,0},{4,5},{5,6},{6,7},{7,4},{8,9},{9,10},{10,1... | collective-permute-start | bytes 983048 | tf_op jit(solution)/shard_map/ppermute | solution.py:20
  184.9 55.5 %collective-permute-start.8 = (bf16[320,768]{1,0:T(8,128)(2,1)}, bf16[320,768]{1,0:T(8,128)(2,1)}, u32[]{:S(2)}, u32[]{:S(2)}) collective-permute-start(bf16[320,768]{1,0:T(8,128)(2,1)} %get-tuple-element.64), channel_id=1, source_target_pairs={{0,3},{1,0},{2,1},{3,2},{4,7},{5,4},{6,5},{7,6},{8,11},{9,8},{10,9... | collective-permute-start | bytes 1474568 | tf_op jit(solution)/shard_map/ppermute | solution.py:20
  186.9 54.0 %collective-permute-start.7 = (bf16[320,768]{1,0:T(8,128)(2,1)}, bf16[320,768]{1,0:T(8,128)(2,1)}, u32[]{:S(2)}, u32[]{:S(2)}) collective-permute-start(bf16[320,768]{1,0:T(8,128)(2,1)} %get-tuple-element.65), channel_id=1, source_target_pairs={{0,2},{1,3},{2,0},{3,1},{4,6},{5,7},{6,4},{7,5},{8,10},{9,11},{10,... | collective-permute-start | bytes 1474568 | tf_op jit(solution)/shard_map/ppermute | solution.py:20
  230.6 5.4 copy-start.16
  230.6 5.4 copy-start.18
  231.6 12.0 %collective-permute-start.6 = (bf16[320,768]{1,0:T(8,128)(2,1)S(1)}, bf16[320,768]{1,0:T(8,128)(2,1)S(1)}, u32[]{:S(2)}, u32[]{:S(2)}) collective-permute-start(bf16[320,768]{1,0:T(8,128)(2,1)S(1)} %copy-done.14), channel_id=1, source_target_pairs={{0,1},{1,2},{2,3},{3,0},{4,5},{5,6},{6,7},{7,4},{8,9},{9,10},{10,1... | collective-permute-start | bytes 1474568 | tf_op jit(solution)/shard_map/ppermute | solution.py:20
  232.9 17.5 %collective-permute-start.5 = (bf16[320,1024]{1,0:T(8,128)(2,1)S(1)}, bf16[320,1024]{1,0:T(8,128)(2,1)S(1)}, u32[]{:S(2)}, u32[]{:S(2)}) collective-permute-start(bf16[320,1024]{1,0:T(8,128)(2,1)S(1)} %get-tuple-element.60), channel_id=1, source_target_pairs={{0,3},{1,0},{2,1},{3,2},{4,7},{5,4},{6,5},{7,6},{8,11},{9,8},{10,9... | collective-permute-start | bytes 1966088 | tf_op jit(solution)/shard_map/ppermute | solution.py:20
  234.3 24.5 %collective-permute-start.4 = (bf16[320,1024]{1,0:T(8,128)(2,1)S(1)}, bf16[320,1024]{1,0:T(8,128)(2,1)S(1)}, u32[]{:S(2)}, u32[]{:S(2)}) collective-permute-start(bf16[320,1024]{1,0:T(8,128)(2,1)S(1)} %get-tuple-element.61), channel_id=1, source_target_pairs={{0,2},{1,3},{2,0},{3,1},{4,6},{5,7},{6,4},{7,5},{8,10},{9,11},{10,... | collective-permute-start | bytes 1966088 | tf_op jit(solution)/shard_map/ppermute | solution.py:20
  236.0 2.3 copy-start.19
  238.3 7.4 %copy-start.13 = (bf16[320,768]{1,0:T(8,128)(2,1)S(1)}, bf16[320,768]{1,0:T(8,128)(2,1)}, u32[]{:S(2)}) copy-start(bf16[320,768]{1,0:T(8,128)(2,1)} %get-tuple-element.63) | copy-start | bytes 1474564
  240.4 32.1 %collective-permute-start.3 = (bf16[320,1024]{1,0:T(8,128)(2,1)S(1)}, bf16[320,1024]{1,0:T(8,128)(2,1)S(1)}, u32[]{:S(2)}, u32[]{:S(2)}) collective-permute-start(bf16[320,1024]{1,0:T(8,128)(2,1)S(1)} %get-tuple-element.62), channel_id=1, source_target_pairs={{0,1},{1,2},{2,3},{3,0},{4,5},{5,6},{6,7},{7,4},{8,9},{9,10},{10,1... | collective-permute-start | bytes 1966088 | tf_op jit(solution)/shard_map/ppermute | solution.py:20
  240.9 37.6 %collective-permute-start.2 = (bf16[320,1280]{1,0:T(8,128)(2,1)S(1)}, bf16[320,1280]{1,0:T(8,128)(2,1)S(1)}, u32[]{:S(2)}, u32[]{:S(2)}) collective-permute-start(bf16[320,1280]{1,0:T(8,128)(2,1)S(1)} %get-tuple-element.52), channel_id=1, source_target_pairs={{0,3},{1,0},{2,1},{3,2},{4,7},{5,4},{6,5},{7,6},{8,11},{9,8},{10,9... | collective-permute-start | bytes 2457608 | tf_op jit(solution)/shard_map/ppermute | solution.py:20
  243.6 46.8 %collective-permute-start.1 = (bf16[320,1280]{1,0:T(8,128)(2,1)S(1)}, bf16[320,1280]{1,0:T(8,128)(2,1)S(1)}, u32[]{:S(2)}, u32[]{:S(2)}) collective-permute-start(bf16[320,1280]{1,0:T(8,128)(2,1)S(1)} %get-tuple-element.53), channel_id=1, source_target_pairs={{0,2},{1,3},{2,0},{3,1},{4,6},{5,7},{6,4},{7,5},{8,10},{9,11},{10,... | collective-permute-start | bytes 2457608 | tf_op jit(solution)/shard_map/ppermute | solution.py:20
  250.5 57.2 %collective-permute-start = (bf16[320,1280]{1,0:T(8,128)(2,1)S(1)}, bf16[320,1280]{1,0:T(8,128)(2,1)S(1)}, u32[]{:S(2)}, u32[]{:S(2)}) collective-permute-start(bf16[320,1280]{1,0:T(8,128)(2,1)S(1)} %get-tuple-element.54), channel_id=1, source_target_pairs={{0,1},{1,2},{2,3},{3,0},{4,5},{5,6},{6,7},{7,4},{8,9},{9,10},{10,1... | collective-permute-start | bytes 2457608 | tf_op jit(solution)/shard_map/ppermute | solution.py:20
  312.3 2.4 copy-start.20
  314.8 10.1 %collective-permute-start.14 = (bf16[320,512]{1,0:T(8,128)(2,1)S(1)}, bf16[320,512]{1,0:T(8,128)(2,1)S(1)}, u32[]{:S(2)}, u32[]{:S(2)}) collective-permute-start(bf16[320,512]{1,0:T(8,128)(2,1)S(1)} %get-tuple-element.56), channel_id=1, source_target_pairs={{0,1},{1,2},{2,3},{3,0},{4,5},{5,6},{6,7},{7,4},{8,9},{9,10},{10,1... | collective-permute-start | bytes 983048 | tf_op jit(solution)/shard_map/ppermute | solution.py:20
  314.8 13.8 %collective-permute-start.13 = (bf16[320,512]{1,0:T(8,128)(2,1)S(1)}, bf16[320,512]{1,0:T(8,128)(2,1)S(1)}, u32[]{:S(2)}, u32[]{:S(2)}) collective-permute-start(bf16[320,512]{1,0:T(8,128)(2,1)S(1)} %get-tuple-element.57), channel_id=1, source_target_pairs={{0,2},{1,3},{2,0},{3,1},{4,6},{5,7},{6,4},{7,5},{8,10},{9,11},{10,... | collective-permute-start | bytes 983048 | tf_op jit(solution)/shard_map/ppermute | solution.py:20
  316.7 15.5 %collective-permute-start.12 = (bf16[320,512]{1,0:T(8,128)(2,1)S(1)}, bf16[320,512]{1,0:T(8,128)(2,1)S(1)}, u32[]{:S(2)}, u32[]{:S(2)}) collective-permute-start(bf16[320,512]{1,0:T(8,128)(2,1)S(1)} %get-tuple-element.58), channel_id=1, source_target_pairs={{0,3},{1,0},{2,1},{3,2},{4,7},{5,4},{6,5},{7,6},{8,11},{9,8},{10,9... | collective-permute-start | bytes 983048 | tf_op jit(solution)/shard_map/ppermute | solution.py:20
  332.9 1.3 copy-start.6
  334.2 11.1 %copy-start.21 = (bf16[1280,512]{1,0:T(8,128)(2,1)S(1)}, bf16[1280,512]{1,0:T(8,128)(2,1)}, u32[]{:S(2)}) copy-start(bf16[1280,512]{1,0:T(8,128)(2,1)} %copy-done.20) | copy-start | bytes 3932164
  336.2 46.1 %all-to-all-start.4 = ((bf16[64,16,512]{2,1,0:T(8,128)(2,1)}), bf16[64,16,512]{2,1,0:T(8,128)(2,1)S(1)}, u32[]{:S(2)}, u32[]{:S(2)}) async-start(bf16[64,16,512]{2,1,0:T(8,128)(2,1)} %bitcast.42), calls=%async_computation.4 | async-start | bytes 2097152 | tf_op jit(solution)/shard_map/all_to_all | solution.py:111
  347.8 13.6 %collective-permute-start.17 = (bf16[320,768]{1,0:T(8,128)(2,1)S(1)}, bf16[320,768]{1,0:T(8,128)(2,1)S(1)}, u32[]{:S(2)}, u32[]{:S(2)}) collective-permute-start(bf16[320,768]{1,0:T(8,128)(2,1)S(1)} %get-tuple-element.48), channel_id=1, source_target_pairs={{0,1},{1,2},{2,3},{3,0},{4,5},{5,6},{6,7},{7,4},{8,9},{9,10},{10,1... | collective-permute-start | bytes 1474568 | tf_op jit(solution)/shard_map/ppermute | solution.py:20
  348.9 23.9 %collective-permute-start.16 = (bf16[320,768]{1,0:T(8,128)(2,1)S(1)}, bf16[320,768]{1,0:T(8,128)(2,1)S(1)}, u32[]{:S(2)}, u32[]{:S(2)}) collective-permute-start(bf16[320,768]{1,0:T(8,128)(2,1)S(1)} %get-tuple-element.49), channel_id=1, source_target_pairs={{0,2},{1,3},{2,0},{3,1},{4,6},{5,7},{6,4},{7,5},{8,10},{9,11},{10,... | collective-permute-start | bytes 1474568 | tf_op jit(solution)/shard_map/ppermute | solution.py:20
  351.4 21.4 %collective-permute-start.15 = (bf16[320,768]{1,0:T(8,128)(2,1)S(1)}, bf16[320,768]{1,0:T(8,128)(2,1)S(1)}, u32[]{:S(2)}, u32[]{:S(2)}) collective-permute-start(bf16[320,768]{1,0:T(8,128)(2,1)S(1)} %get-tuple-element.50), channel_id=1, source_target_pairs={{0,3},{1,0},{2,1},{3,2},{4,7},{5,4},{6,5},{7,6},{8,11},{9,8},{10,9... | collective-permute-start | bytes 1474568 | tf_op jit(solution)/shard_map/ppermute | solution.py:20
  378.3 1.3 copy-start.7
  382.3 12.3 %copy-start.22 = (bf16[1280,512]{1,0:T(8,128)(2,1)S(1)}, bf16[1280,512]{1,0:T(8,128)(2,1)}, u32[]{:S(2)}) copy-start(bf16[1280,512]{1,0:T(8,128)(2,1)} %copy-done.20) | copy-start | bytes 3932164
  383.3 57.8 %all-to-all-start.5 = ((bf16[64,16,768]{2,1,0:T(8,128)(2,1)}), bf16[64,16,768]{2,1,0:T(8,128)(2,1)S(1)}, u32[]{:S(2)}, u32[]{:S(2)}) async-start(bf16[64,16,768]{2,1,0:T(8,128)(2,1)} %bitcast.177), calls=%async_computation.5 | async-start | bytes 3145728 | tf_op jit(solution)/shard_map/all_to_all | solution.py:111
  397.5 17.3 %collective-permute-start.20 = (bf16[320,1024]{1,0:T(8,128)(2,1)S(1)}, bf16[320,1024]{1,0:T(8,128)(2,1)S(1)}, u32[]{:S(2)}, u32[]{:S(2)}) collective-permute-start(bf16[320,1024]{1,0:T(8,128)(2,1)S(1)} %get-tuple-element.44), channel_id=1, source_target_pairs={{0,1},{1,2},{2,3},{3,0},{4,5},{5,6},{6,7},{7,4},{8,9},{9,10},{10,1... | collective-permute-start | bytes 1966088 | tf_op jit(solution)/shard_map/ppermute | solution.py:20
  398.6 30.9 %collective-permute-start.19 = (bf16[320,1024]{1,0:T(8,128)(2,1)S(1)}, bf16[320,1024]{1,0:T(8,128)(2,1)S(1)}, u32[]{:S(2)}, u32[]{:S(2)}) collective-permute-start(bf16[320,1024]{1,0:T(8,128)(2,1)S(1)} %get-tuple-element.45), channel_id=1, source_target_pairs={{0,2},{1,3},{2,0},{3,1},{4,6},{5,7},{6,4},{7,5},{8,10},{9,11},{10,... | collective-permute-start | bytes 1966088 | tf_op jit(solution)/shard_map/ppermute | solution.py:20
  401.1 28.4 %collective-permute-start.18 = (bf16[320,1024]{1,0:T(8,128)(2,1)S(1)}, bf16[320,1024]{1,0:T(8,128)(2,1)S(1)}, u32[]{:S(2)}, u32[]{:S(2)}) collective-permute-start(bf16[320,1024]{1,0:T(8,128)(2,1)S(1)} %get-tuple-element.46), channel_id=1, source_target_pairs={{0,3},{1,0},{2,1},{3,2},{4,7},{5,4},{6,5},{7,6},{8,11},{9,8},{10,9... | collective-permute-start | bytes 1966088 | tf_op jit(solution)/shard_map/ppermute | solution.py:20
  436.6 1.3 copy-start.8
  442.3 67.4 %all-to-all-start.6 = ((bf16[64,16,1024]{2,1,0:T(8,128)(2,1)}), bf16[64,16,1024]{2,1,0:T(8,128)(2,1)S(1)}, u32[]{:S(2)}, u32[]{:S(2)}) async-start(bf16[64,16,1024]{2,1,0:T(8,128)(2,1)} %bitcast.175), calls=%async_computation.6 | async-start | bytes 4194304 | tf_op jit(solution)/shard_map/all_to_all | solution.py:111
  457.3 20.6 %collective-permute-start.23 = (bf16[320,1280]{1,0:T(8,128)(2,1)S(1)}, bf16[320,1280]{1,0:T(8,128)(2,1)S(1)}, u32[]{:S(2)}, u32[]{:S(2)}) collective-permute-start(bf16[320,1280]{1,0:T(8,128)(2,1)S(1)} %get-tuple-element.40), channel_id=1, source_target_pairs={{0,1},{1,2},{2,3},{3,0},{4,5},{5,6},{6,7},{7,4},{8,9},{9,10},{10,1... | collective-permute-start | bytes 2457608 | tf_op jit(solution)/shard_map/ppermute | solution.py:20
  458.2 38.2 %collective-permute-start.22 = (bf16[320,1280]{1,0:T(8,128)(2,1)S(1)}, bf16[320,1280]{1,0:T(8,128)(2,1)S(1)}, u32[]{:S(2)}, u32[]{:S(2)}) collective-permute-start(bf16[320,1280]{1,0:T(8,128)(2,1)S(1)} %get-tuple-element.41), channel_id=1, source_target_pairs={{0,2},{1,3},{2,0},{3,1},{4,6},{5,7},{6,4},{7,5},{8,10},{9,11},{10,... | collective-permute-start | bytes 2457608 | tf_op jit(solution)/shard_map/ppermute | solution.py:20
  460.9 35.4 %collective-permute-start.21 = (bf16[320,1280]{1,0:T(8,128)(2,1)S(1)}, bf16[320,1280]{1,0:T(8,128)(2,1)S(1)}, u32[]{:S(2)}, u32[]{:S(2)}) collective-permute-start(bf16[320,1280]{1,0:T(8,128)(2,1)S(1)} %get-tuple-element.42), channel_id=1, source_target_pairs={{0,3},{1,0},{2,1},{3,2},{4,7},{5,4},{6,5},{7,6},{8,11},{9,8},{10,9... | collective-permute-start | bytes 2457608 | tf_op jit(solution)/shard_map/ppermute | solution.py:20
  509.7 1.4 copy-start
  511.0 72.1 %all-to-all-start.7 = ((bf16[64,16,1280]{2,1,0:T(8,128)(2,1)}), bf16[64,16,1280]{2,1,0:T(8,128)(2,1)S(1)}, u32[]{:S(2)}, u32[]{:S(2)}) async-start(bf16[64,16,1280]{2,1,0:T(8,128)(2,1)} %bitcast.172), calls=%async_computation.7 | async-start | bytes 5242880 | tf_op jit(solution)/shard_map/all_to_all | solution.py:111
  522.3 3.6 copy-start.1
  (7 other events, 7.8 us)

commit v3 on v2

--- a/solution.py
+++ b/solution.py
@@ -3,8 +3,8 @@
 from jax import lax
 from jax.sharding import PartitionSpec as P
 
-GO_UNITS = (10, 8, 6, 4)
-RET_UNITS = (4, 6, 8, 10)
+GO_UNITS = (12, 12, 4)
+RET_UNITS = (4, 8, 8, 8)
 
 
 def bounds(units, width):
@@ -97,6 +97,10 @@
 
     outs = []
     owner = ((here + device_line) % n_local) // 2 == jnp.arange(per_group, dtype=jnp.int32)[:, None]
+    gated = pick.reshape(arrived_count, per_group, expert_cap) * expert_gates.astype(jnp.bfloat16)[None]
+    comb = jnp.concatenate(
+        [jnp.sum(jnp.where(owner[None, :, j, None], gated, 0.0), axis=1) for j in range(n_local)], axis=1
+    ).astype(jnp.bfloat16)
     for cols in bounds(RET_UNITS, width):
         chunk = cols.stop - cols.start
         partial_value = jnp.dot(hidden, w_down[:, cols], preferred_element_type=jnp.float32)
@@ -104,10 +108,8 @@
         by_shift = [partial_value[0]] + [
             shifted(partial_value[shift], (n_local - shift) % n_local) for shift in range(1, n_local)
         ]
-        stacked, owner_c, gates_c, pick_c = lax.optimization_barrier((jnp.stack(by_shift), owner, expert_gates, pick))
-        summed = jnp.sum(jnp.where(owner_c[:, :, None, None], stacked.astype(jnp.float32)[None], 0.0), axis=1)
-        term = (gates_c[:, :, None] * summed).astype(jnp.bfloat16)
-        group_part = one_hot_dot(pick_c, term.reshape(per_group * expert_cap, chunk), "ak,kd->ad")
+        stacked, comb_c = lax.optimization_barrier((jnp.concatenate(by_shift, axis=0), comb))
+        group_part = one_hot_dot(comb_c, stacked, "ak,kd->ad")
         back = lax.all_to_all(
             group_part.reshape(n_groups, send_cap, chunk), "group", split_axis=0, concat_axis=0, tiled=True
         ).reshape(arrived_count, chunk)

time: 596 us -> 571 us (0.958)
  other arithmetic: 29.7 us -> 9.19 us
  starting transfers between devices: 107 us -> 89 us
  waiting for transfers between devices: 368 us -> 383 us
    ppermute x24 -> x21, waiting for transfers between devices: 153 us -> 164 us  [shifted(): lax.ppermute(array, 'local', [(i, (i + shift) % n_local) for i in range(n...]
    reduce_sum x4 -> x0, other arithmetic: 11.4 us -> none  [local(): jnp.sum(jnp.where(owner_c[:, :, None, None], stacked.astype(jnp.float32)[...]
    convert_element_type x9 -> x0, other arithmetic: 11.1 us -> none  [the longest x4 8.86 us: local(): stacked.astype(jnp.float32)[None]]
    ppermute x24 -> x21, starting transfers between devices: 31.5 us -> 25 us  [shifted(): lax.ppermute(array, 'local', [(i, (i + shift) % n_local) for i in range(n...]
    all_to_all x4 -> x3, starting transfers between devices: 32.8 us -> 26.8 us  [local(): lax.all_to_all(rows_out, 'group', split_axis=0, concat_axis=0, tiled=True)]
    unnamed x52 -> x34, local copies, waits for them, and re-layouts: 12.9 us -> 8.46 us
    dot_general x16 -> x14, matrix products: 32.8 us -> 36.6 us  [one_hot_dot(): jnp.einsum(spec, select, values, preferred_element_type=jnp.float32)]
    all_to_all x4 -> x3, waiting for transfers between devices: 159 us -> 157 us  [local(): lax.all_to_all(rows_out, 'group', split_axis=0, concat_axis=0, tiled=True)]
  transfers between devices with their start and end apart: 32 -> 28, of which waited for: 20 -> 23; matrix products, arithmetic and copies ran while one was open for 14% -> 11% of each run, Pallas kernels for 0% -> 0%
where the time goes in v3:
time: 571 us; the launch traced here: 561 us
  waiting for transfers between devices  383 us (67%)
  starting transfers between devices  89 us (16%)
  matrix products  64.1 us (11%)
  local copies, waits for them, and re-layouts  14.8 us (3%)
  other arithmetic  9.19 us (2%)
    ppermute x21, waiting for transfers between devices, shifted(): lax.ppermute(array, 'local', [(i, (i + shift) % n_local) for i in range(n...  164 us
    all_to_all x3, waiting for transfers between devices, local(): lax.all_to_all(rows_out, 'group', split_axis=0, concat_axis=0, tiled=True)  157 us
    all_to_all x4, waiting for transfers between devices, local(): lax.all_to_all(group_part.reshape(n_groups, send_cap, chunk), 'group', sp...  61.4 us
    all_to_all x4, starting transfers between devices, local(): lax.all_to_all(group_part.reshape(n_groups, send_cap, chunk), 'group', sp...  37.3 us
    dot_general x14, matrix products, one_hot_dot(): jnp.einsum(spec, select, values, preferred_element_type=jnp.float32)  36.6 us
    all_to_all x3, starting transfers between devices, local(): lax.all_to_all(rows_out, 'group', split_axis=0, concat_axis=0, tiled=True)  26.8 us
    ppermute x21, starting transfers between devices, shifted(): lax.ppermute(array, 'local', [(i, (i + shift) % n_local) for i in range(n...  25 us
    dot_general x4, matrix products, local(): jnp.dot(hidden, w_down[:, cols], preferred_element_type=jnp.float32)  11.7 us
  transfers between devices with their start and end apart: 28, of which 23 were waited for; matrix products, arithmetic and copies ran while one was open for 11% of the time, Pallas kernels for 0%

profile of v3, /device:TPU:1, one launch (start us, length us, event | category | flops | bytes accessed | tf_op | source)
XLA Modules:
  0.0 560.8 jit_solution(1905944321827537415)
XLA Ops:
  8.4 13.0 %all-to-all-start = ((bf16[64,16,1664]{2,1,0:T(8,128)(2,1)}), bf16[64,16,1664]{2,1,0:T(8,128)(2,1)S(1)}, u32[]{:S(2)}, u32[]{:S(2)}) async-start(bf16[64,16,1664]{2,1,0:T(8,128)(2,1)} %fusion.2), calls=%async_computation | async-start | bytes 6815744 | tf_op jit(solution)/shard_map/all_to_all | solution.py:81
  21.3 3.6 convolution_convert_fusion.3
  24.9 74.4 %all-to-all-done = bf16[64,16,1664]{2,1,0:T(8,128)(2,1)S(1)} async-done(((bf16[64,16,1664]{2,1,0:T(8,128)(2,1)}), bf16[64,16,1664]{2,1,0:T(8,128)(2,1)S(1)}, u32[]{:S(2)}, u32[]{:S(2)}) %all-to-all-start) | async-done | bytes 3407904 | tf_op jit(solution)/shard_map/all_to_all | solution.py:81
  99.3 7.1 %all-to-all-start.1 = ((bf16[64,16,1536]{2,1,0:T(8,128)(2,1)}), bf16[64,16,1536]{2,1,0:T(8,128)(2,1)}, u32[]{:S(2)}, u32[]{:S(2)}) async-start(bf16[64,16,1536]{2,1,0:T(8,128)(2,1)} %bitcast.117), calls=%async_computation.1 | async-start | bytes 6291456 | tf_op jit(solution)/shard_map/all_to_all | solution.py:81
  107.2 2.2 convolution_convert_fusion.12
  111.3 67.8 %all-to-all-done.1 = bf16[64,16,1536]{2,1,0:T(8,128)(2,1)} async-done(((bf16[64,16,1536]{2,1,0:T(8,128)(2,1)}), bf16[64,16,1536]{2,1,0:T(8,128)(2,1)}, u32[]{:S(2)}, u32[]{:S(2)}) %all-to-all-start.1) | async-done | bytes 3145760 | tf_op jit(solution)/shard_map/all_to_all | solution.py:81
  179.1 6.7 %all-to-all-start.2 = ((bf16[64,16,512]{2,1,0:T(8,128)(2,1)}), bf16[64,16,512]{2,1,0:T(8,128)(2,1)}, u32[]{:S(2)}, u32[]{:S(2)}) async-start(bf16[64,16,512]{2,1,0:T(8,128)(2,1)} %bitcast.121), calls=%async_computation.2 | async-start | bytes 2097152 | tf_op jit(solution)/shard_map/all_to_all | solution.py:81
  187.4 4.3 convolution_convert_fusion.5
  195.0 2.6 collective-permute-start.4
  198.8 15.0 %all-to-all-done.2 = bf16[64,16,512]{2,1,0:T(8,128)(2,1)} async-done(((bf16[64,16,512]{2,1,0:T(8,128)(2,1)}), bf16[64,16,512]{2,1,0:T(8,128)(2,1)}, u32[]{:S(2)}, u32[]{:S(2)}) %all-to-all-start.2) | async-done | bytes 1048608 | tf_op jit(solution)/shard_map/all_to_all | solution.py:81
  213.9 2.3 convolution_convert_fusion.13
  217.6 2.6 collective-permute-start.7
  220.7 2.2 convolution_convert_fusion.6
  222.9 2.3 select_reduce_fusion.4
  225.3 22.1 %collective-permute-done.6 = bf16[320,512]{1,0:T(8,128)(2,1)S(1)} collective-permute-done((bf16[320,512]{1,0:T(8,128)(2,1)S(1)}, bf16[320,512]{1,0:T(8,128)(2,1)S(1)}, u32[]{:S(2)}, u32[]{:S(2)}) %collective-permute-start.6) | collective-permute-done | bytes 327712 | tf_op jit(solution)/shard_map/ppermute | solution.py:20
  247.8 6.5 %collective-permute-done.7 = bf16[320,512]{1,0:T(8,128)(2,1)S(1)} collective-permute-done((bf16[320,512]{1,0:T(8,128)(2,1)S(1)}, bf16[320,512]{1,0:T(8,128)(2,1)S(1)}, u32[]{:S(2)}, u32[]{:S(2)}) %collective-permute-start.7) | collective-permute-done | bytes 327712 | tf_op jit(solution)/shard_map/ppermute | solution.py:20
  255.2 3.3 collective-permute-start.1
  262.1 4.6 fusion.10
  266.7 4.6 fusion.15
  271.4 27.1 %collective-permute-done = bf16[320,1536]{1,0:T(8,128)(2,1)S(1)} collective-permute-done((bf16[320,1536]{1,0:T(8,128)(2,1)S(1)}, bf16[320,1536]{1,0:T(8,128)(2,1)S(1)}, u32[]{:S(2)}, u32[]{:S(2)}) %collective-permute-start) | collective-permute-done | bytes 983072 | tf_op jit(solution)/shard_map/ppermute | solution.py:20
  299.8 2.2 fusion.3
  302.0 2.6 multiply_convert_fusion
  304.7 2.3 convolution_convert_fusion.7
  307.1 2.6 collective-permute-start.10
  312.9 3.6 collective-permute-done.10
  316.4 8.9 %collective-permute-done.11 = bf16[320,512]{1,0:T(8,128)(2,1)S(1)} collective-permute-done((bf16[320,512]{1,0:T(8,128)(2,1)S(1)}, bf16[320,512]{1,0:T(8,128)(2,1)S(1)}, u32[]{:S(2)}, u32[]{:S(2)}) %collective-permute-start.11) | collective-permute-done | bytes 327712 | tf_op jit(solution)/shard_map/ppermute | solution.py:20
  325.6 2.6 convolution_convert_fusion.11
  328.2 11.9 %all-to-all-start.3 = ((bf16[64,16,512]{2,1,0:T(8,128)(2,1)}), bf16[64,16,512]{2,1,0:T(8,128)(2,1)S(1)}, u32[]{:S(2)}, u32[]{:S(2)}) async-start(bf16[64,16,512]{2,1,0:T(8,128)(2,1)} %bitcast.127), calls=%async_computation.3 | async-start | bytes 2097152 | tf_op jit(solution)/shard_map/all_to_all | solution.py:113
  340.1 3.1 convolution_convert_fusion.2
  343.5 2.4 collective-permute-start.12
  346.6 13.7 %collective-permute-done.12 = bf16[320,1024]{1,0:T(8,128)(2,1)S(1)} collective-permute-done((bf16[320,1024]{1,0:T(8,128)(2,1)S(1)}, bf16[320,1024]{1,0:T(8,128)(2,1)S(1)}, u32[]{:S(2)}, u32[]{:S(2)}) %collective-permute-start.12) | collective-permute-done | bytes 655392 | tf_op jit(solution)/shard_map/ppermute | solution.py:20
  360.3 2.8 collective-permute-done.13
  363.2 14.4 %collective-permute-done.14 = bf16[320,1024]{1,0:T(8,128)(2,1)S(1)} collective-permute-done((bf16[320,1024]{1,0:T(8,128)(2,1)S(1)}, bf16[320,1024]{1,0:T(8,128)(2,1)S(1)}, u32[]{:S(2)}, u32[]{:S(2)}) %collective-permute-start.14) | collective-permute-done | bytes 655392 | tf_op jit(solution)/shard_map/ppermute | solution.py:20
  379.3 4.2 convolution_convert_fusion.10
  383.5 10.7 %all-to-all-start.4 = ((bf16[64,16,1024]{2,1,0:T(8,128)(2,1)}), bf16[64,16,1024]{2,1,0:T(8,128)(2,1)S(1)}, u32[]{:S(2)}, u32[]{:S(2)}) async-start(bf16[64,16,1024]{2,1,0:T(8,128)(2,1)} %bitcast.125), calls=%async_computation.4 | async-start | bytes 4194304 | tf_op jit(solution)/shard_map/all_to_all | solution.py:113
  394.2 3.1 convolution_convert_fusion.1
  399.2 14.4 %collective-permute-done.15 = bf16[320,1024]{1,0:T(8,128)(2,1)S(1)} collective-permute-done((bf16[320,1024]{1,0:T(8,128)(2,1)S(1)}, bf16[320,1024]{1,0:T(8,128)(2,1)S(1)}, u32[]{:S(2)}, u32[]{:S(2)}) %collective-permute-start.15) | collective-permute-done | bytes 655392 | tf_op jit(solution)/shard_map/ppermute | solution.py:20
  415.4 15.1 %collective-permute-done.17 = bf16[320,1024]{1,0:T(8,128)(2,1)S(1)} collective-permute-done((bf16[320,1024]{1,0:T(8,128)(2,1)S(1)}, bf16[320,1024]{1,0:T(8,128)(2,1)S(1)}, u32[]{:S(2)}, u32[]{:S(2)}) %collective-permute-start.17) | collective-permute-done | bytes 655392 | tf_op jit(solution)/shard_map/ppermute | solution.py:20
  432.2 4.1 convolution_convert_fusion.9
  436.4 7.5 %all-to-all-done.4 = bf16[64,16,1024]{2,1,0:T(8,128)(2,1)S(1)} async-done(((bf16[64,16,1024]{2,1,0:T(8,128)(2,1)}), bf16[64,16,1024]{2,1,0:T(8,128)(2,1)S(1)}, u32[]{:S(2)}, u32[]{:S(2)}) %all-to-all-start.4) | async-done | bytes 2097184 | tf_op jit(solution)/shard_map/all_to_all | solution.py:113
  443.9 7.5 %all-to-all-start.5 = ((bf16[64,16,1024]{2,1,0:T(8,128)(2,1)}), bf16[64,16,1024]{2,1,0:T(8,128)(2,1)}, u32[]{:S(2)}, u32[]{:S(2)}) async-start(bf16[64,16,1024]{2,1,0:T(8,128)(2,1)} %bitcast.124), calls=%async_computation.5 | async-start | bytes 4194304 | tf_op jit(solution)/shard_map/all_to_all | solution.py:113
  451.4 3.1 convolution_convert_fusion
  456.4 14.6 %collective-permute-done.18 = bf16[320,1024]{1,0:T(8,128)(2,1)S(1)} collective-permute-done((bf16[320,1024]{1,0:T(8,128)(2,1)S(1)}, bf16[320,1024]{1,0:T(8,128)(2,1)S(1)}, u32[]{:S(2)}, u32[]{:S(2)}) %collective-permute-start.18) | collective-permute-done | bytes 655392 | tf_op jit(solution)/shard_map/ppermute | solution.py:20
  472.8 14.9 %collective-permute-done.20 = bf16[320,1024]{1,0:T(8,128)(2,1)S(1)} collective-permute-done((bf16[320,1024]{1,0:T(8,128)(2,1)S(1)}, bf16[320,1024]{1,0:T(8,128)(2,1)S(1)}, u32[]{:S(2)}, u32[]{:S(2)}) %collective-permute-start.20) | collective-permute-done | bytes 655392 | tf_op jit(solution)/shard_map/ppermute | solution.py:20
  489.5 4.2 convolution_convert_fusion.8
  493.7 7.2 %all-to-all-done.5 = bf16[64,16,1024]{2,1,0:T(8,128)(2,1)} async-done(((bf16[64,16,1024]{2,1,0:T(8,128)(2,1)}), bf16[64,16,1024]{2,1,0:T(8,128)(2,1)}, u32[]{:S(2)}, u32[]{:S(2)}) %all-to-all-start.5) | async-done | bytes 2097184 | tf_op jit(solution)/shard_map/all_to_all | solution.py:113
  500.9 7.2 %all-to-all-start.6 = ((bf16[64,16,1024]{2,1,0:T(8,128)(2,1)}), bf16[64,16,1024]{2,1,0:T(8,128)(2,1)}, u32[]{:S(2)}, u32[]{:S(2)}) async-start(bf16[64,16,1024]{2,1,0:T(8,128)(2,1)} %bitcast.126), calls=%async_computation.6 | async-start | bytes 4194304 | tf_op jit(solution)/shard_map/all_to_all | solution.py:113
  511.0 46.6 %all-to-all-done.6 = bf16[64,16,1024]{2,1,0:T(8,128)(2,1)} async-done(((bf16[64,16,1024]{2,1,0:T(8,128)(2,1)}), bf16[64,16,1024]{2,1,0:T(8,128)(2,1)}, u32[]{:S(2)}, u32[]{:S(2)}) %all-to-all-start.6) | async-done | bytes 2097184 | tf_op jit(solution)/shard_map/all_to_all | solution.py:113
  (118 shorter events, 47.8 us)
Async XLA Ops:
  1.6 2.7 copy-start.4
  8.4 91.0 %all-to-all-start = ((bf16[64,16,1664]{2,1,0:T(8,128)(2,1)}), bf16[64,16,1664]{2,1,0:T(8,128)(2,1)S(1)}, u32[]{:S(2)}, u32[]{:S(2)}) async-start(bf16[64,16,1664]{2,1,0:T(8,128)(2,1)} %fusion.2), calls=%async_computation | async-start | bytes 6815744 | tf_op jit(solution)/shard_map/all_to_all | solution.py:81
  99.3 79.7 %all-to-all-start.1 = ((bf16[64,16,1536]{2,1,0:T(8,128)(2,1)}), bf16[64,16,1536]{2,1,0:T(8,128)(2,1)}, u32[]{:S(2)}, u32[]{:S(2)}) async-start(bf16[64,16,1536]{2,1,0:T(8,128)(2,1)} %bitcast.117), calls=%async_computation.1 | async-start | bytes 6291456 | tf_op jit(solution)/shard_map/all_to_all | solution.py:81
  179.1 34.8 %all-to-all-start.2 = ((bf16[64,16,512]{2,1,0:T(8,128)(2,1)}), bf16[64,16,512]{2,1,0:T(8,128)(2,1)}, u32[]{:S(2)}, u32[]{:S(2)}) async-start(bf16[64,16,512]{2,1,0:T(8,128)(2,1)} %bitcast.121), calls=%async_computation.2 | async-start | bytes 2097152 | tf_op jit(solution)/shard_map/all_to_all | solution.py:81
  187.3 4.3 copy-start.7
  193.7 67.7 %collective-permute-start.3 = (bf16[320,1536]{1,0:T(8,128)(2,1)}, bf16[320,1536]{1,0:T(8,128)(2,1)}, u32[]{:S(2)}, u32[]{:S(2)}) collective-permute-start(bf16[320,1536]{1,0:T(8,128)(2,1)} %get-tuple-element.46), channel_id=1, source_target_pairs={{0,1},{1,2},{2,3},{3,0},{4,5},{5,6},{6,7},{7,4},{8,9},{9,10},{10,1... | collective-permute-start | bytes 2949128 | tf_op jit(solution)/shard_map/ppermute | solution.py:20
  195.0 67.1 %collective-permute-start.4 = (bf16[320,1536]{1,0:T(8,128)(2,1)}, bf16[320,1536]{1,0:T(8,128)(2,1)}, u32[]{:S(2)}, u32[]{:S(2)}) collective-permute-start(bf16[320,1536]{1,0:T(8,128)(2,1)} %get-tuple-element.45), channel_id=1, source_target_pairs={{0,2},{1,3},{2,0},{3,1},{4,6},{5,7},{6,4},{7,5},{8,10},{9,11},{10,... | collective-permute-start | bytes 2949128 | tf_op jit(solution)/shard_map/ppermute | solution.py:20
  197.6 64.5 %collective-permute-start.5 = (bf16[320,1536]{1,0:T(8,128)(2,1)}, bf16[320,1536]{1,0:T(8,128)(2,1)}, u32[]{:S(2)}, u32[]{:S(2)}) collective-permute-start(bf16[320,1536]{1,0:T(8,128)(2,1)} %get-tuple-element.44), channel_id=1, source_target_pairs={{0,3},{1,0},{2,1},{3,2},{4,7},{5,4},{6,5},{7,6},{8,11},{9,8},{10,9... | collective-permute-start | bytes 2949128 | tf_op jit(solution)/shard_map/ppermute | solution.py:20
  216.3 31.1 %collective-permute-start.6 = (bf16[320,512]{1,0:T(8,128)(2,1)S(1)}, bf16[320,512]{1,0:T(8,128)(2,1)S(1)}, u32[]{:S(2)}, u32[]{:S(2)}) collective-permute-start(bf16[320,512]{1,0:T(8,128)(2,1)S(1)} %get-tuple-element.54), channel_id=1, source_target_pairs={{0,1},{1,2},{2,3},{3,0},{4,5},{5,6},{6,7},{7,4},{8,9},{9,10},{10,1... | collective-permute-start | bytes 983048 | tf_op jit(solution)/shard_map/ppermute | solution.py:20
  217.6 3.0 copy-start.8
  217.6 36.7 %collective-permute-start.7 = (bf16[320,512]{1,0:T(8,128)(2,1)S(1)}, bf16[320,512]{1,0:T(8,128)(2,1)S(1)}, u32[]{:S(2)}, u32[]{:S(2)}) collective-permute-start(bf16[320,512]{1,0:T(8,128)(2,1)S(1)} %get-tuple-element.53), channel_id=1, source_target_pairs={{0,2},{1,3},{2,0},{3,1},{4,6},{5,7},{6,4},{7,5},{8,10},{9,11},{10,... | collective-permute-start | bytes 983048 | tf_op jit(solution)/shard_map/ppermute | solution.py:20
  220.7 2.2 copy-start.9
  220.7 2.2 copy-start.10
  247.4 7.9 %collective-permute-start.8 = (bf16[320,512]{1,0:T(8,128)(2,1)S(1)}, bf16[320,512]{1,0:T(8,128)(2,1)S(1)}, u32[]{:S(2)}, u32[]{:S(2)}) collective-permute-start(bf16[320,512]{1,0:T(8,128)(2,1)S(1)} %get-tuple-element.52), channel_id=1, source_target_pairs={{0,3},{1,0},{2,1},{3,2},{4,7},{5,4},{6,5},{7,6},{8,11},{9,8},{10,9... | collective-permute-start | bytes 983048 | tf_op jit(solution)/shard_map/ppermute | solution.py:20
  247.5 11.0 %copy-start.12 = (bf16[3584,512]{1,0:T(8,128)(2,1)S(1)}, bf16[3584,512]{1,0:T(8,128)(2,1)}, u32[]{:S(2)}) copy-start(bf16[3584,512]{1,0:T(8,128)(2,1)} %param.10) | copy-start | bytes 11010052
  254.3 44.2 %collective-permute-start = (bf16[320,1536]{1,0:T(8,128)(2,1)S(1)}, bf16[320,1536]{1,0:T(8,128)(2,1)S(1)}, u32[]{:S(2)}, u32[]{:S(2)}) collective-permute-start(bf16[320,1536]{1,0:T(8,128)(2,1)S(1)} %get-tuple-element.42), channel_id=1, source_target_pairs={{0,1},{1,2},{2,3},{3,0},{4,5},{5,6},{6,7},{7,4},{8,9},{9,10},{10,1... | collective-permute-start | bytes 2949128 | tf_op jit(solution)/shard_map/ppermute | solution.py:20
  255.2 43.3 %collective-permute-start.1 = (bf16[320,1536]{1,0:T(8,128)(2,1)S(1)}, bf16[320,1536]{1,0:T(8,128)(2,1)S(1)}, u32[]{:S(2)}, u32[]{:S(2)}) collective-permute-start(bf16[320,1536]{1,0:T(8,128)(2,1)S(1)} %get-tuple-element.41), channel_id=1, source_target_pairs={{0,2},{1,3},{2,0},{3,1},{4,6},{5,7},{6,4},{7,5},{8,10},{9,11},{10,... | collective-permute-start | bytes 2949128 | tf_op jit(solution)/shard_map/ppermute | solution.py:20
  258.5 2.0 copy-start.11
  260.6 1.6 copy-start.6
  261.4 38.4 %collective-permute-start.2 = (bf16[320,1536]{1,0:T(8,128)(2,1)S(1)}, bf16[320,1536]{1,0:T(8,128)(2,1)S(1)}, u32[]{:S(2)}, u32[]{:S(2)}) collective-permute-start(bf16[320,1536]{1,0:T(8,128)(2,1)S(1)} %get-tuple-element.40), channel_id=1, source_target_pairs={{0,3},{1,0},{2,1},{3,2},{4,7},{5,4},{6,5},{7,6},{8,11},{9,8},{10,9... | collective-permute-start | bytes 2949128 | tf_op jit(solution)/shard_map/ppermute | solution.py:20
  304.6 2.4 copy-start.13
  307.1 9.3 %collective-permute-start.10 = (bf16[320,512]{1,0:T(8,128)(2,1)S(1)}, bf16[320,512]{1,0:T(8,128)(2,1)S(1)}, u32[]{:S(2)}, u32[]{:S(2)}) collective-permute-start(bf16[320,512]{1,0:T(8,128)(2,1)S(1)} %get-tuple-element.49), channel_id=1, source_target_pairs={{0,2},{1,3},{2,0},{3,1},{4,6},{5,7},{6,4},{7,5},{8,10},{9,11},{10,... | collective-permute-start | bytes 983048 | tf_op jit(solution)/shard_map/ppermute | solution.py:20
  309.7 15.6 %collective-permute-start.11 = (bf16[320,512]{1,0:T(8,128)(2,1)S(1)}, bf16[320,512]{1,0:T(8,128)(2,1)S(1)}, u32[]{:S(2)}, u32[]{:S(2)}) collective-permute-start(bf16[320,512]{1,0:T(8,128)(2,1)S(1)} %get-tuple-element.48), channel_id=1, source_target_pairs={{0,1},{1,2},{2,3},{3,0},{4,5},{5,6},{6,7},{7,4},{8,9},{9,10},{10,1... | collective-permute-start | bytes 983048 | tf_op jit(solution)/shard_map/ppermute | solution.py:20
  311.2 14.4 %collective-permute-start.9 = (bf16[320,512]{1,0:T(8,128)(2,1)S(1)}, bf16[320,512]{1,0:T(8,128)(2,1)S(1)}, u32[]{:S(2)}, u32[]{:S(2)}) collective-permute-start(bf16[320,512]{1,0:T(8,128)(2,1)S(1)} %get-tuple-element.50), channel_id=1, source_target_pairs={{0,3},{1,0},{2,1},{3,2},{4,7},{5,4},{6,5},{7,6},{8,11},{9,8},{10,9... | collective-permute-start | bytes 983048 | tf_op jit(solution)/shard_map/ppermute | solution.py:20
  312.9 15.3 %copy-start = (bf16[1024,1280]{0,1:T(8,128)(2,1)}, bf16[1024,1280]{0,1:T(8,128)(2,1)S(1)}, u32[]{:S(2)}) copy-start(bf16[1024,1280]{0,1:T(8,128)(2,1)S(1)} %pad_maximum_fusion.2) | copy-start | bytes 7864324
  328.2 55.3 %all-to-all-start.3 = ((bf16[64,16,512]{2,1,0:T(8,128)(2,1)}), bf16[64,16,512]{2,1,0:T(8,128)(2,1)S(1)}, u32[]{:S(2)}, u32[]{:S(2)}) async-start(bf16[64,16,512]{2,1,0:T(8,128)(2,1)} %bitcast.127), calls=%async_computation.3 | async-start | bytes 2097152 | tf_op jit(solution)/shard_map/all_to_all | solution.py:113
  343.5 16.8 %collective-permute-start.12 = (bf16[320,1024]{1,0:T(8,128)(2,1)S(1)}, bf16[320,1024]{1,0:T(8,128)(2,1)S(1)}, u32[]{:S(2)}, u32[]{:S(2)}) collective-permute-start(bf16[320,1024]{1,0:T(8,128)(2,1)S(1)} %get-tuple-element.30), channel_id=1, source_target_pairs={{0,3},{1,0},{2,1},{3,2},{4,7},{5,4},{6,5},{7,6},{8,11},{9,8},{10,9... | collective-permute-start | bytes 1966088 | tf_op jit(solution)/shard_map/ppermute | solution.py:20
  345.9 17.3 %collective-permute-start.13 = (bf16[320,1024]{1,0:T(8,128)(2,1)S(1)}, bf16[320,1024]{1,0:T(8,128)(2,1)S(1)}, u32[]{:S(2)}, u32[]{:S(2)}) collective-permute-start(bf16[320,1024]{1,0:T(8,128)(2,1)S(1)} %get-tuple-element.29), channel_id=1, source_target_pairs={{0,2},{1,3},{2,0},{3,1},{4,6},{5,7},{6,4},{7,5},{8,10},{9,11},{10,... | collective-permute-start | bytes 1966088 | tf_op jit(solution)/shard_map/ppermute | solution.py:20
  345.9 31.6 %collective-permute-start.14 = (bf16[320,1024]{1,0:T(8,128)(2,1)S(1)}, bf16[320,1024]{1,0:T(8,128)(2,1)S(1)}, u32[]{:S(2)}, u32[]{:S(2)}) collective-permute-start(bf16[320,1024]{1,0:T(8,128)(2,1)S(1)} %get-tuple-element.28), channel_id=1, source_target_pairs={{0,1},{1,2},{2,3},{3,0},{4,5},{5,6},{6,7},{7,4},{8,9},{9,10},{10,1... | collective-permute-start | bytes 1966088 | tf_op jit(solution)/shard_map/ppermute | solution.py:20
  377.6 1.7 copy-start.1
  383.5 60.4 %all-to-all-start.4 = ((bf16[64,16,1024]{2,1,0:T(8,128)(2,1)}), bf16[64,16,1024]{2,1,0:T(8,128)(2,1)S(1)}, u32[]{:S(2)}, u32[]{:S(2)}) async-start(bf16[64,16,1024]{2,1,0:T(8,128)(2,1)} %bitcast.125), calls=%async_computation.4 | async-start | bytes 4194304 | tf_op jit(solution)/shard_map/all_to_all | solution.py:113
  397.6 15.9 %collective-permute-start.15 = (bf16[320,1024]{1,0:T(8,128)(2,1)S(1)}, bf16[320,1024]{1,0:T(8,128)(2,1)S(1)}, u32[]{:S(2)}, u32[]{:S(2)}) collective-permute-start(bf16[320,1024]{1,0:T(8,128)(2,1)S(1)} %get-tuple-element.34), channel_id=1, source_target_pairs={{0,3},{1,0},{2,1},{3,2},{4,7},{5,4},{6,5},{7,6},{8,11},{9,8},{10,9... | collective-permute-start | bytes 1966088 | tf_op jit(solution)/shard_map/ppermute | solution.py:20
  398.3 17.1 %collective-permute-start.16 = (bf16[320,1024]{1,0:T(8,128)(2,1)S(1)}, bf16[320,1024]{1,0:T(8,128)(2,1)S(1)}, u32[]{:S(2)}, u32[]{:S(2)}) collective-permute-start(bf16[320,1024]{1,0:T(8,128)(2,1)S(1)} %get-tuple-element.33), channel_id=1, source_target_pairs={{0,2},{1,3},{2,0},{3,1},{4,6},{5,7},{6,4},{7,5},{8,10},{9,11},{10,... | collective-permute-start | bytes 1966088 | tf_op jit(solution)/shard_map/ppermute | solution.py:20
  398.3 32.2 %collective-permute-start.17 = (bf16[320,1024]{1,0:T(8,128)(2,1)S(1)}, bf16[320,1024]{1,0:T(8,128)(2,1)S(1)}, u32[]{:S(2)}, u32[]{:S(2)}) collective-permute-start(bf16[320,1024]{1,0:T(8,128)(2,1)S(1)} %get-tuple-element.32), channel_id=1, source_target_pairs={{0,1},{1,2},{2,3},{3,0},{4,5},{5,6},{6,7},{7,4},{8,9},{9,10},{10,1... | collective-permute-start | bytes 1966088 | tf_op jit(solution)/shard_map/ppermute | solution.py:20
  430.5 1.7 copy-start.2
  443.9 56.9 %all-to-all-start.5 = ((bf16[64,16,1024]{2,1,0:T(8,128)(2,1)}), bf16[64,16,1024]{2,1,0:T(8,128)(2,1)}, u32[]{:S(2)}, u32[]{:S(2)}) async-start(bf16[64,16,1024]{2,1,0:T(8,128)(2,1)} %bitcast.124), calls=%async_computation.5 | async-start | bytes 4194304 | tf_op jit(solution)/shard_map/all_to_all | solution.py:113
  454.8 16.1 %collective-permute-start.18 = (bf16[320,1024]{1,0:T(8,128)(2,1)S(1)}, bf16[320,1024]{1,0:T(8,128)(2,1)S(1)}, u32[]{:S(2)}, u32[]{:S(2)}) collective-permute-start(bf16[320,1024]{1,0:T(8,128)(2,1)S(1)} %get-tuple-element.38), channel_id=1, source_target_pairs={{0,3},{1,0},{2,1},{3,2},{4,7},{5,4},{6,5},{7,6},{8,11},{9,8},{10,9... | collective-permute-start | bytes 1966088 | tf_op jit(solution)/shard_map/ppermute | solution.py:20
  455.5 17.3 %collective-permute-start.19 = (bf16[320,1024]{1,0:T(8,128)(2,1)S(1)}, bf16[320,1024]{1,0:T(8,128)(2,1)S(1)}, u32[]{:S(2)}, u32[]{:S(2)}) collective-permute-start(bf16[320,1024]{1,0:T(8,128)(2,1)S(1)} %get-tuple-element.37), channel_id=1, source_target_pairs={{0,2},{1,3},{2,0},{3,1},{4,6},{5,7},{6,4},{7,5},{8,10},{9,11},{10,... | collective-permute-start | bytes 1966088 | tf_op jit(solution)/shard_map/ppermute | solution.py:20
  455.5 32.2 %collective-permute-start.20 = (bf16[320,1024]{1,0:T(8,128)(2,1)S(1)}, bf16[320,1024]{1,0:T(8,128)(2,1)S(1)}, u32[]{:S(2)}, u32[]{:S(2)}) collective-permute-start(bf16[320,1024]{1,0:T(8,128)(2,1)S(1)} %get-tuple-element.36), channel_id=1, source_target_pairs={{0,1},{1,2},{2,3},{3,0},{4,5},{5,6},{6,7},{7,4},{8,9},{9,10},{10,1... | collective-permute-start | bytes 1966088 | tf_op jit(solution)/shard_map/ppermute | solution.py:20
  487.7 1.7 copy-start.3
  493.7 14.4 %copy-start.5 = (s32[64,64]{0,1:T(8,128)S(1)}, s32[64,64]{0,1:T(8,128)}, u32[]{:S(2)}) copy-start(s32[64,64]{0,1:T(8,128)} %copy-done.4) | copy-start | bytes 49156
  500.9 56.8 %all-to-all-start.6 = ((bf16[64,16,1024]{2,1,0:T(8,128)(2,1)}), bf16[64,16,1024]{2,1,0:T(8,128)(2,1)}, u32[]{:S(2)}, u32[]{:S(2)}) async-start(bf16[64,16,1024]{2,1,0:T(8,128)(2,1)} %bitcast.126), calls=%async_computation.6 | async-start | bytes 4194304 | tf_op jit(solution)/shard_map/all_to_all | solution.py:113

commit v4 on v3

--- a/solution.py
+++ b/solution.py
@@ -3,7 +3,7 @@
 from jax import lax
 from jax.sharding import PartitionSpec as P
 
-GO_UNITS = (12, 12, 4)
+GO_UNITS = (8, 8, 8, 4)
 RET_UNITS = (4, 8, 8, 8)
 
 
@@ -82,11 +82,17 @@
         if c == 0:
             expert_gates, pick = route(rows_in[:, :, chunk:])
         rows_in = rows_in[:, :, :chunk].reshape(arrived_count, chunk)
-        expert_rows = one_hot_dot(pick, rows_in, "ak,ad->kd").reshape(per_group, expert_cap, chunk)
+        if c == 0:
+            owner = ((here + device_line) % n_local) // 2 == jnp.arange(per_group, dtype=jnp.int32)[:, None]
+            pick3 = pick.reshape(arrived_count, per_group, expert_cap)
+            by_dest = jnp.concatenate(
+                [jnp.sum(jnp.where(owner[None, :, j, None], pick3, 0.0), axis=1) for j in range(n_local)],
+                axis=1,
+            ).astype(jnp.bfloat16)
+        dest_rows = one_hot_dot(by_dest, rows_in, "ak,ad->kd").reshape(n_local, expert_cap, chunk)
         blocks = []
         for shift in range(n_local):
-            dest_expert = ((here + shift) % n_local) // 2
-            block = lax.dynamic_index_in_dim(expert_rows, dest_expert, 0, keepdims=False)
+            block = dest_rows[shift]
             blocks.append(block if shift == 0 else shifted(block, shift))
         flat_rows = jnp.concatenate(blocks, axis=0)
         g_part = jnp.dot(flat_rows, w_gate[cols, :], preferred_element_type=jnp.float32)

time: 571 us -> 592 us (1.037)
  starting transfers between devices: 89 us -> 106 us
  matrix products: 64.1 us -> 79.7 us
  waiting for transfers between devices: 383 us -> 371 us
    ppermute x21 -> x24, starting transfers between devices: 25 us -> 37.8 us  [shifted(): lax.ppermute(array, 'local', [(i, (i + shift) % n_local) for i in range(n...]
    dot_general x14 -> x16, matrix products: 36.6 us -> 48.7 us  [one_hot_dot(): jnp.einsum(spec, select, values, preferred_element_type=jnp.float32)]
    all_to_all x3 -> x4, waiting for transfers between devices: 157 us -> 150 us  [local(): lax.all_to_all(rows_out, 'group', split_axis=0, concat_axis=0, tiled=True)]
    all_to_all x3 -> x4, starting transfers between devices: 26.8 us -> 33.7 us  [local(): lax.all_to_all(rows_out, 'group', split_axis=0, concat_axis=0, tiled=True)]
    ppermute x21 -> x24, waiting for transfers between devices: 164 us -> 158 us  [shifted(): lax.ppermute(array, 'local', [(i, (i + shift) % n_local) for i in range(n...]
    dot_general x3 -> x4, matrix products: 8.09 us -> 12.8 us  [local(): jnp.dot(flat_rows, w_up[cols, :], preferred_element_type=jnp.float32)]
  transfers between devices with their start and end apart: 28 -> 32, of which waited for: 23 -> 24; matrix products, arithmetic and copies ran while one was open for 11% -> 13% of each run, Pallas kernels for 0% -> 0%
where the time goes in v4:
time: 592 us; the launch traced here: 584 us
  waiting for transfers between devices  371 us (63%)
  starting transfers between devices  106 us (18%)
  matrix products  79.7 us (13%)
  local copies, waits for them, and re-layouts  13.8 us (2%)
  other arithmetic  13.4 us (2%)
    ppermute x24, waiting for transfers between devices, shifted(): lax.ppermute(array, 'local', [(i, (i + shift) % n_local) for i in range(n...  158 us
    all_to_all x4, waiting for transfers between devices, local(): lax.all_to_all(rows_out, 'group', split_axis=0, concat_axis=0, tiled=True)  150 us
    all_to_all x4, waiting for transfers between devices, local(): lax.all_to_all(group_part.reshape(n_groups, send_cap, chunk), 'group', sp...  62.8 us
    dot_general x16, matrix products, one_hot_dot(): jnp.einsum(spec, select, values, preferred_element_type=jnp.float32)  48.7 us
    ppermute x24, starting transfers between devices, shifted(): lax.ppermute(array, 'local', [(i, (i + shift) % n_local) for i in range(n...  37.8 us
    all_to_all x4, starting transfers between devices, local(): lax.all_to_all(group_part.reshape(n_groups, send_cap, chunk), 'group', sp...  34.1 us
    all_to_all x4, starting transfers between devices, local(): lax.all_to_all(rows_out, 'group', split_axis=0, concat_axis=0, tiled=True)  33.7 us
    dot_general x4, matrix products, local(): jnp.dot(flat_rows, w_up[cols, :], preferred_element_type=jnp.float32)  12.8 us
  transfers between devices with their start and end apart: 32, of which 24 were waited for; matrix products, arithmetic and copies ran while one was open for 13% of the time, Pallas kernels for 0%

profile of v4, /device:TPU:1, one launch (start us, length us, event | category | flops | bytes accessed | tf_op | source)
XLA Modules:
  0.0 584.3 jit_solution(3165660098988223160)
XLA Ops:
  4.1 13.0 %all-to-all-start.3 = ((bf16[64,16,512]{2,1,0:T(8,128)(2,1)}), bf16[64,16,512]{2,1,0:T(8,128)(2,1)S(1)}, u32[]{:S(2)}, u32[]{:S(2)}) async-start(bf16[64,16,512]{2,1,0:T(8,128)(2,1)} %bitcast.16), calls=%async_computation.3 | async-start | bytes 2097152 | tf_op jit(solution)/shard_map/all_to_all | solution.py:81
  19.1 26.1 %all-to-all-done.3 = bf16[64,16,512]{2,1,0:T(8,128)(2,1)S(1)} async-done(((bf16[64,16,512]{2,1,0:T(8,128)(2,1)}), bf16[64,16,512]{2,1,0:T(8,128)(2,1)S(1)}, u32[]{:S(2)}, u32[]{:S(2)}) %all-to-all-start.3) | async-done | bytes 1048608 | tf_op jit(solution)/shard_map/all_to_all | solution.py:81
  46.2 6.3 %all-to-all-start.1 = ((bf16[64,16,1024]{2,1,0:T(8,128)(2,1)}), bf16[64,16,1024]{2,1,0:T(8,128)(2,1)S(1)}, u32[]{:S(2)}, u32[]{:S(2)}) async-start(bf16[64,16,1024]{2,1,0:T(8,128)(2,1)} %bitcast.12), calls=%async_computation.1 | async-start | bytes 4194304 | tf_op jit(solution)/shard_map/all_to_all | solution.py:81
  56.9 45.3 %all-to-all-done.1 = bf16[64,16,1024]{2,1,0:T(8,128)(2,1)S(1)} async-done(((bf16[64,16,1024]{2,1,0:T(8,128)(2,1)}), bf16[64,16,1024]{2,1,0:T(8,128)(2,1)S(1)}, u32[]{:S(2)}, u32[]{:S(2)}) %all-to-all-start.1) | async-done | bytes 2097184 | tf_op jit(solution)/shard_map/all_to_all | solution.py:81
  103.6 7.0 %all-to-all-start = ((bf16[64,16,1152]{2,1,0:T(8,128)(2,1)}), bf16[64,16,1152]{2,1,0:T(8,128)(2,1)S(1)}, u32[]{:S(2)}, u32[]{:S(2)}) async-start(bf16[64,16,1152]{2,1,0:T(8,128)(2,1)} %fusion.11), calls=%async_computation | async-start | bytes 4718592 | tf_op jit(solution)/shard_map/all_to_all | solution.py:81
  112.6 53.3 %all-to-all-done = bf16[64,16,1152]{2,1,0:T(8,128)(2,1)S(1)} async-done(((bf16[64,16,1152]{2,1,0:T(8,128)(2,1)}), bf16[64,16,1152]{2,1,0:T(8,128)(2,1)S(1)}, u32[]{:S(2)}, u32[]{:S(2)}) %all-to-all-start) | async-done | bytes 2359328 | tf_op jit(solution)/shard_map/all_to_all | solution.py:81
  165.9 7.5 %all-to-all-start.2 = ((bf16[64,16,1024]{2,1,0:T(8,128)(2,1)}), bf16[64,16,1024]{2,1,0:T(8,128)(2,1)}, u32[]{:S(2)}, u32[]{:S(2)}) async-start(bf16[64,16,1024]{2,1,0:T(8,128)(2,1)} %bitcast.90), calls=%async_computation.2 | async-start | bytes 4194304 | tf_op jit(solution)/shard_map/all_to_all | solution.py:81
  174.9 7.1 %fusion.21 = (bf16[1024,320]{0,1:T(8,128)(2,1)S(1)}, bf16[1024,320]{0,1:T(8,128)(2,1)S(1)}, bf16[1024,320]{0,1:T(8,128)(2,1)S(1)}, bf16[1024,320]{0,1:T(8,128)(2...) fusion(s32[1024,2]{0,1:T(2,128)S(1)} %bitcast.101, ...), kind=kOutput, calls=%fused_computation.46 | output fusion | flops 13108863 | bytes 5261320 | tf_op jit(solution)/shard_map/reduce_sum | solution.py:65
  182.1 4.1 convolution_convert_fusion.7
  187.2 2.7 collective-permute-start.11
  191.4 6.7 %convolution_convert_fusion.4 = bf16[1280,1024]{1,0:T(8,128)(2,1)} fusion(bf16[1024,1024]{1,0:T(8,128)(2,1)S(1)} %bitcast.92, bf16[1024,320]{0,1:T(8,128)(2,1)S(1)} %get-tuple-element.26, bf16[1024,320]{0,1:T(8,128)(2,1)S(1)} %get-tuple-element.27, bf16[1024,320]{0,1:T(8,128)(2,1)S(1)} %get-tuple-element.28, bf16[1024,320]{0,1:T(8,128)(2,1)S(1)} %get-tuple-element.25), kind=kOutput, calls=%fused_computation.7 | convolution fusion | flops 2696151040 | bytes 7340032 | tf_op jit(solution)/shard_map/ak,ad->kd/dot_general | solution.py:24
  198.1 24.8 %all-to-all-done.2 = bf16[64,16,1024]{2,1,0:T(8,128)(2,1)} async-done(((bf16[64,16,1024]{2,1,0:T(8,128)(2,1)}), bf16[64,16,1024]{2,1,0:T(8,128)(2,1)}, u32[]{:S(2)}, u32[]{:S(2)}) %all-to-all-start.2) | async-done | bytes 2097184 | tf_op jit(solution)/shard_map/all_to_all | solution.py:81
  222.9 5.3 convolution_convert_fusion.3
  229.9 5.5 convolution_convert_fusion.5
  235.9 2.8 collective-permute-start.5
  248.0 3.8 collective-permute-done.5
  254.3 12.4 %collective-permute-start.2 = (bf16[320,1024]{1,0:T(8,128)(2,1)S(1)}, bf16[320,1024]{1,0:T(8,128)(2,1)S(1)}, u32[]{:S(2)}, u32[]{:S(2)}) collective-permute-start(bf16[320,1024]{1,0:T(8,128)(2,1)S(1)} %get-tuple-element.48), channel_id=1, source_target_pairs={{0,3},{1,0},{2,1},{3,2},{4,7},{5,4},{6,5},{7,6},{8,11},{9,8},{10,9... | collective-permute-start | bytes 1966088 | tf_op jit(solution)/shard_map/ppermute | solution.py:20
  266.7 6.9 %collective-permute-done.3 = bf16[320,1024]{1,0:T(8,128)(2,1)S(1)} collective-permute-done((bf16[320,1024]{1,0:T(8,128)(2,1)S(1)}, bf16[320,1024]{1,0:T(8,128)(2,1)S(1)}, u32[]{:S(2)}, u32[]{:S(2)}) %collective-permute-start.3) | collective-permute-done | bytes 655392 | tf_op jit(solution)/shard_map/ppermute | solution.py:20
  277.0 2.8 collective-permute-done.8
  279.8 2.5 collective-permute-done.7
  282.4 19.2 %collective-permute-done.6 = bf16[320,1024]{1,0:T(8,128)(2,1)S(1)} collective-permute-done((bf16[320,1024]{1,0:T(8,128)(2,1)S(1)}, bf16[320,1024]{1,0:T(8,128)(2,1)S(1)}, u32[]{:S(2)}, u32[]{:S(2)}) %collective-permute-start.6) | collective-permute-done | bytes 655392 | tf_op jit(solution)/shard_map/ppermute | solution.py:20
  301.5 3.0 fusion.36
  307.9 2.6 collective-permute-done.1
  310.5 16.5 %collective-permute-done = bf16[320,1024]{1,0:T(8,128)(2,1)S(1)} collective-permute-done((bf16[320,1024]{1,0:T(8,128)(2,1)S(1)}, bf16[320,1024]{1,0:T(8,128)(2,1)S(1)}, u32[]{:S(2)}, u32[]{:S(2)}) %collective-permute-start) | collective-permute-done | bytes 655392 | tf_op jit(solution)/shard_map/ppermute | solution.py:20
  328.7 6.1 %multiply_convert_fusion = bf16[1280,512]{1,0:T(8,128)(2,1)S(1)} fusion(f32[1280,512]{1,0:T(8,128)S(1)} %fusion.5, f32[1280,512]{1,0:T(8,128)S(1)} %fusion.49, f32[1280,512]{1,0:T(8,128)} %fusion.36, f32[1280,512]{1,0:T(8,128)S(1)} %fusion.38, bf16[3584,512]{1,0:T(8,128)(2,1)S(1)} %copy-done.15, bf16[320,1024]{1,0:T(8,128)(2,1)S(1)} %collective-permute-done.2, ...), kind=kOutput, calls=%fused_computation.27 | convolution fusion | flops 1358561280 | bytes 15466496 | tf_op jit(solution)/shard_map/dot_general | solution.py:99
  340.5 13.9 %collective-permute-done.14 = bf16[320,512]{1,0:T(8,128)(2,1)S(1)} collective-permute-done((bf16[320,512]{1,0:T(8,128)(2,1)S(1)}, bf16[320,512]{1,0:T(8,128)(2,1)S(1)}, u32[]{:S(2)}, u32[]{:S(2)}) %collective-permute-start.14) | collective-permute-done | bytes 327712 | tf_op jit(solution)/shard_map/ppermute | solution.py:20
  357.4 8.2 %all-to-all-start.4 = ((bf16[64,16,512]{2,1,0:T(8,128)(2,1)}), bf16[64,16,512]{2,1,0:T(8,128)(2,1)S(1)}, u32[]{:S(2)}, u32[]{:S(2)}) async-start(bf16[64,16,512]{2,1,0:T(8,128)(2,1)} %bitcast.18), calls=%async_computation.4 | async-start | bytes 2097152 | tf_op jit(solution)/shard_map/all_to_all | solution.py:119
  365.6 2.7 convolution_convert_fusion
  368.7 3.2 collective-permute-start.22
  371.9 13.9 %collective-permute-done.23 = bf16[320,1024]{1,0:T(8,128)(2,1)S(1)} collective-permute-done((bf16[320,1024]{1,0:T(8,128)(2,1)S(1)}, bf16[320,1024]{1,0:T(8,128)(2,1)S(1)}, u32[]{:S(2)}, u32[]{:S(2)}) %collective-permute-start.23) | collective-permute-done | bytes 655392 | tf_op jit(solution)/shard_map/ppermute | solution.py:20
  385.8 14.6 %collective-permute-done.22 = bf16[320,1024]{1,0:T(8,128)(2,1)S(1)} collective-permute-done((bf16[320,1024]{1,0:T(8,128)(2,1)S(1)}, bf16[320,1024]{1,0:T(8,128)(2,1)S(1)}, u32[]{:S(2)}, u32[]{:S(2)}) %collective-permute-start.22) | collective-permute-done | bytes 655392 | tf_op jit(solution)/shard_map/ppermute | solution.py:20
  402.2 4.1 convolution_convert_fusion.8
  406.3 11.2 %all-to-all-start.7 = ((bf16[64,16,1024]{2,1,0:T(8,128)(2,1)}), bf16[64,16,1024]{2,1,0:T(8,128)(2,1)S(1)}, u32[]{:S(2)}, u32[]{:S(2)}) async-start(bf16[64,16,1024]{2,1,0:T(8,128)(2,1)} %bitcast.94), calls=%async_computation.7 | async-start | bytes 4194304 | tf_op jit(solution)/shard_map/all_to_all | solution.py:119
  417.5 3.1 convolution_convert_fusion.1
  420.9 3.5 collective-permute-start.19
  424.5 13.5 %collective-permute-done.20 = bf16[320,1024]{1,0:T(8,128)(2,1)S(1)} collective-permute-done((bf16[320,1024]{1,0:T(8,128)(2,1)S(1)}, bf16[320,1024]{1,0:T(8,128)(2,1)S(1)}, u32[]{:S(2)}, u32[]{:S(2)}) %collective-permute-start.20) | collective-permute-done | bytes 655392 | tf_op jit(solution)/shard_map/ppermute | solution.py:20
  438.0 14.9 %collective-permute-done.19 = bf16[320,1024]{1,0:T(8,128)(2,1)S(1)} collective-permute-done((bf16[320,1024]{1,0:T(8,128)(2,1)S(1)}, bf16[320,1024]{1,0:T(8,128)(2,1)S(1)}, u32[]{:S(2)}, u32[]{:S(2)}) %collective-permute-start.19) | collective-permute-done | bytes 655392 | tf_op jit(solution)/shard_map/ppermute | solution.py:20
  454.6 4.2 convolution_convert_fusion.9
  458.8 8.3 %all-to-all-done.7 = bf16[64,16,1024]{2,1,0:T(8,128)(2,1)S(1)} async-done(((bf16[64,16,1024]{2,1,0:T(8,128)(2,1)}), bf16[64,16,1024]{2,1,0:T(8,128)(2,1)S(1)}, u32[]{:S(2)}, u32[]{:S(2)}) %all-to-all-start.7) | async-done | bytes 2097184 | tf_op jit(solution)/shard_map/all_to_all | solution.py:119
  467.2 7.6 %all-to-all-start.6 = ((bf16[64,16,1024]{2,1,0:T(8,128)(2,1)}), bf16[64,16,1024]{2,1,0:T(8,128)(2,1)}, u32[]{:S(2)}, u32[]{:S(2)}) async-start(bf16[64,16,1024]{2,1,0:T(8,128)(2,1)} %bitcast.93), calls=%async_computation.6 | async-start | bytes 4194304 | tf_op jit(solution)/shard_map/all_to_all | solution.py:119
  474.8 3.1 convolution_convert_fusion.2
  478.2 3.5 collective-permute-start.16
  481.8 13.7 %collective-permute-done.17 = bf16[320,1024]{1,0:T(8,128)(2,1)S(1)} collective-permute-done((bf16[320,1024]{1,0:T(8,128)(2,1)S(1)}, bf16[320,1024]{1,0:T(8,128)(2,1)S(1)}, u32[]{:S(2)}, u32[]{:S(2)}) %collective-permute-start.17) | collective-permute-done | bytes 655392 | tf_op jit(solution)/shard_map/ppermute | solution.py:20
  495.5 14.9 %collective-permute-done.16 = bf16[320,1024]{1,0:T(8,128)(2,1)S(1)} collective-permute-done((bf16[320,1024]{1,0:T(8,128)(2,1)S(1)}, bf16[320,1024]{1,0:T(8,128)(2,1)S(1)}, u32[]{:S(2)}, u32[]{:S(2)}) %collective-permute-start.16) | collective-permute-done | bytes 655392 | tf_op jit(solution)/shard_map/ppermute | solution.py:20
  512.1 4.2 convolution_convert_fusion.10
  516.3 7.8 %all-to-all-done.6 = bf16[64,16,1024]{2,1,0:T(8,128)(2,1)} async-done(((bf16[64,16,1024]{2,1,0:T(8,128)(2,1)}), bf16[64,16,1024]{2,1,0:T(8,128)(2,1)}, u32[]{:S(2)}, u32[]{:S(2)}) %all-to-all-start.6) | async-done | bytes 2097184 | tf_op jit(solution)/shard_map/all_to_all | solution.py:119
  524.2 7.2 %all-to-all-start.5 = ((bf16[64,16,1024]{2,1,0:T(8,128)(2,1)}), bf16[64,16,1024]{2,1,0:T(8,128)(2,1)}, u32[]{:S(2)}, u32[]{:S(2)}) async-start(bf16[64,16,1024]{2,1,0:T(8,128)(2,1)} %bitcast.95), calls=%async_computation.5 | async-start | bytes 4194304 | tf_op jit(solution)/shard_map/all_to_all | solution.py:119
  534.3 46.7 %all-to-all-done.5 = bf16[64,16,1024]{2,1,0:T(8,128)(2,1)} async-done(((bf16[64,16,1024]{2,1,0:T(8,128)(2,1)}), bf16[64,16,1024]{2,1,0:T(8,128)(2,1)}, u32[]{:S(2)}, u32[]{:S(2)}) %all-to-all-start.5) | async-done | bytes 2097184 | tf_op jit(solution)/shard_map/all_to_all | solution.py:119
  (152 shorter events, 61.6 us)
Async XLA Ops:
  0.0 17.1 %copy-start.12 = (bf16[64,3584]{1,0:T(8,128)(2,1)S(1)}, bf16[64,3584]{1,0:T(8,128)(2,1)}, u32[]{:S(2)}) copy-start(bf16[64,3584]{1,0:T(8,128)(2,1)} %param.6) | copy-start | bytes 1376260
  4.1 41.1 %all-to-all-start.3 = ((bf16[64,16,512]{2,1,0:T(8,128)(2,1)}), bf16[64,16,512]{2,1,0:T(8,128)(2,1)S(1)}, u32[]{:S(2)}, u32[]{:S(2)}) async-start(bf16[64,16,512]{2,1,0:T(8,128)(2,1)} %bitcast.16), calls=%async_computation.3 | async-start | bytes 2097152 | tf_op jit(solution)/shard_map/all_to_all | solution.py:81
  19.1 33.5 %copy-start.13 = (f32[64,8]{0,1:T(8,128)S(1)}, f32[64,8]{0,1:T(8,128)}, u32[]{:S(2)}) copy-start(f32[64,8]{0,1:T(8,128)} %param.8) | copy-start | bytes 6148
  46.2 56.0 %all-to-all-start.1 = ((bf16[64,16,1024]{2,1,0:T(8,128)(2,1)}), bf16[64,16,1024]{2,1,0:T(8,128)(2,1)S(1)}, u32[]{:S(2)}, u32[]{:S(2)}) async-start(bf16[64,16,1024]{2,1,0:T(8,128)(2,1)} %bitcast.12), calls=%async_computation.1 | async-start | bytes 4194304 | tf_op jit(solution)/shard_map/all_to_all | solution.py:81
  103.6 62.3 %all-to-all-start = ((bf16[64,16,1152]{2,1,0:T(8,128)(2,1)}), bf16[64,16,1152]{2,1,0:T(8,128)(2,1)S(1)}, u32[]{:S(2)}, u32[]{:S(2)}) async-start(bf16[64,16,1152]{2,1,0:T(8,128)(2,1)} %fusion.11), calls=%async_computation | async-start | bytes 4718592 | tf_op jit(solution)/shard_map/all_to_all | solution.py:81
  165.9 57.0 %all-to-all-start.2 = ((bf16[64,16,1024]{2,1,0:T(8,128)(2,1)}), bf16[64,16,1024]{2,1,0:T(8,128)(2,1)}, u32[]{:S(2)}, u32[]{:S(2)}) async-start(bf16[64,16,1024]{2,1,0:T(8,128)(2,1)} %bitcast.90), calls=%async_computation.2 | async-start | bytes 4194304 | tf_op jit(solution)/shard_map/all_to_all | solution.py:81
  174.9 7.1 %copy-start.8 = (bf16[64,16,512]{2,1,0:T(8,128)(2,1)S(1)}, bf16[64,16,512]{2,1,0:T(8,128)(2,1)}, u32[]{:S(2)}) copy-start(bf16[64,16,512]{2,1,0:T(8,128)(2,1)} %copy-done.7) | copy-start | bytes 3145732
  182.0 9.3 %copy-start.17 = (bf16[1024,320]{0,1:T(8,128)(2,1)}, bf16[1024,320]{0,1:T(8,128)(2,1)S(1)}, u32[]{:S(2)}) copy-start(bf16[1024,320]{0,1:T(8,128)(2,1)S(1)} %get-tuple-element.25) | copy-start | bytes 1966084
  182.1 9.3 %copy-start.19 = (bf16[1024,320]{0,1:T(8,128)(2,1)}, bf16[1024,320]{0,1:T(8,128)(2,1)S(1)}, u32[]{:S(2)}) copy-start(bf16[1024,320]{0,1:T(8,128)(2,1)S(1)} %get-tuple-element.26) | copy-start | bytes 1966084
  182.1 9.3 %copy-start.21 = (bf16[1024,320]{0,1:T(8,128)(2,1)}, bf16[1024,320]{0,1:T(8,128)(2,1)S(1)}, u32[]{:S(2)}) copy-start(bf16[1024,320]{0,1:T(8,128)(2,1)S(1)} %get-tuple-element.27) | copy-start | bytes 1966084
  182.1 9.4 %copy-start.23 = (bf16[1024,320]{0,1:T(8,128)(2,1)}, bf16[1024,320]{0,1:T(8,128)(2,1)S(1)}, u32[]{:S(2)}) copy-start(bf16[1024,320]{0,1:T(8,128)(2,1)S(1)} %get-tuple-element.28) | copy-start | bytes 1966084
  186.2 5.2 copy-start.6
  187.2 51.9 %collective-permute-start.11 = (bf16[320,512]{1,0:T(8,128)(2,1)}, bf16[320,512]{1,0:T(8,128)(2,1)}, u32[]{:S(2)}, u32[]{:S(2)}) collective-permute-start(bf16[320,512]{1,0:T(8,128)(2,1)} %get-tuple-element.64), channel_id=1, source_target_pairs={{0,3},{1,0},{2,1},{3,2},{4,7},{5,4},{6,5},{7,6},{8,11},{9,8},{10,9... | collective-permute-start | bytes 983048 | tf_op jit(solution)/shard_map/ppermute | solution.py:20
  189.9 50.1 %collective-permute-start.10 = (bf16[320,512]{1,0:T(8,128)(2,1)}, bf16[320,512]{1,0:T(8,128)(2,1)}, u32[]{:S(2)}, u32[]{:S(2)}) collective-permute-start(bf16[320,512]{1,0:T(8,128)(2,1)} %get-tuple-element.65), channel_id=1, source_target_pairs={{0,2},{1,3},{2,0},{3,1},{4,6},{5,7},{6,4},{7,5},{8,10},{9,11},{10,... | collective-permute-start | bytes 983048 | tf_op jit(solution)/shard_map/ppermute | solution.py:20
  190.2 51.9 %collective-permute-start.9 = (bf16[320,512]{1,0:T(8,128)(2,1)}, bf16[320,512]{1,0:T(8,128)(2,1)}, u32[]{:S(2)}, u32[]{:S(2)}) collective-permute-start(bf16[320,512]{1,0:T(8,128)(2,1)} %get-tuple-element.66), channel_id=1, source_target_pairs={{0,1},{1,2},{2,3},{3,0},{4,5},{5,6},{6,7},{7,4},{8,9},{9,10},{10,1... | collective-permute-start | bytes 983048 | tf_op jit(solution)/shard_map/ppermute | solution.py:20
  229.9 5.6 copy-start.4
  235.9 15.9 %collective-permute-start.5 = (bf16[320,1024]{1,0:T(8,128)(2,1)S(1)}, bf16[320,1024]{1,0:T(8,128)(2,1)S(1)}, u32[]{:S(2)}, u32[]{:S(2)}) collective-permute-start(bf16[320,1024]{1,0:T(8,128)(2,1)S(1)} %get-tuple-element.52), channel_id=1, source_target_pairs={{0,3},{1,0},{2,1},{3,2},{4,7},{5,4},{6,5},{7,6},{8,11},{9,8},{10,9... | collective-permute-start | bytes 1966088 | tf_op jit(solution)/shard_map/ppermute | solution.py:20
  238.7 15.5 %collective-permute-start.4 = (bf16[320,1024]{1,0:T(8,128)(2,1)S(1)}, bf16[320,1024]{1,0:T(8,128)(2,1)S(1)}, u32[]{:S(2)}, u32[]{:S(2)}) collective-permute-start(bf16[320,1024]{1,0:T(8,128)(2,1)S(1)} %get-tuple-element.53), channel_id=1, source_target_pairs={{0,2},{1,3},{2,0},{3,1},{4,6},{5,7},{6,4},{7,5},{8,10},{9,11},{10,... | collective-permute-start | bytes 1966088 | tf_op jit(solution)/shard_map/ppermute | solution.py:20
  239.1 4.6 copy-start.15
  239.1 34.5 %collective-permute-start.3 = (bf16[320,1024]{1,0:T(8,128)(2,1)S(1)}, bf16[320,1024]{1,0:T(8,128)(2,1)S(1)}, u32[]{:S(2)}, u32[]{:S(2)}) collective-permute-start(bf16[320,1024]{1,0:T(8,128)(2,1)S(1)} %get-tuple-element.54), channel_id=1, source_target_pairs={{0,1},{1,2},{2,3},{3,0},{4,5},{5,6},{6,7},{7,4},{8,9},{9,10},{10,1... | collective-permute-start | bytes 1966088 | tf_op jit(solution)/shard_map/ppermute | solution.py:20
  240.1 39.8 %collective-permute-start.8 = (bf16[320,1024]{1,0:T(8,128)(2,1)S(1)}, bf16[320,1024]{1,0:T(8,128)(2,1)S(1)}, u32[]{:S(2)}, u32[]{:S(2)}) collective-permute-start(bf16[320,1024]{1,0:T(8,128)(2,1)S(1)} %get-tuple-element.56), channel_id=1, source_target_pairs={{0,3},{1,0},{2,1},{3,2},{4,7},{5,4},{6,5},{7,6},{8,11},{9,8},{10,9... | collective-permute-start | bytes 1966088 | tf_op jit(solution)/shard_map/ppermute | solution.py:20
  242.1 40.3 %collective-permute-start.7 = (bf16[320,1024]{1,0:T(8,128)(2,1)S(1)}, bf16[320,1024]{1,0:T(8,128)(2,1)S(1)}, u32[]{:S(2)}, u32[]{:S(2)}) collective-permute-start(bf16[320,1024]{1,0:T(8,128)(2,1)S(1)} %get-tuple-element.57), channel_id=1, source_target_pairs={{0,2},{1,3},{2,0},{3,1},{4,6},{5,7},{6,4},{7,5},{8,10},{9,11},{10,... | collective-permute-start | bytes 1966088 | tf_op jit(solution)/shard_map/ppermute | solution.py:20
  243.7 2.3 copy-start.14
  251.8 49.7 %collective-permute-start.6 = (bf16[320,1024]{1,0:T(8,128)(2,1)S(1)}, bf16[320,1024]{1,0:T(8,128)(2,1)S(1)}, u32[]{:S(2)}, u32[]{:S(2)}) collective-permute-start(bf16[320,1024]{1,0:T(8,128)(2,1)S(1)} %get-tuple-element.58), channel_id=1, source_target_pairs={{0,1},{1,2},{2,3},{3,0},{4,5},{5,6},{6,7},{7,4},{8,9},{9,10},{10,1... | collective-permute-start | bytes 1966088 | tf_op jit(solution)/shard_map/ppermute | solution.py:20
  254.3 53.6 %collective-permute-start.2 = (bf16[320,1024]{1,0:T(8,128)(2,1)S(1)}, bf16[320,1024]{1,0:T(8,128)(2,1)S(1)}, u32[]{:S(2)}, u32[]{:S(2)}) collective-permute-start(bf16[320,1024]{1,0:T(8,128)(2,1)S(1)} %get-tuple-element.48), channel_id=1, source_target_pairs={{0,3},{1,0},{2,1},{3,2},{4,7},{5,4},{6,5},{7,6},{8,11},{9,8},{10,9... | collective-permute-start | bytes 1966088 | tf_op jit(solution)/shard_map/ppermute | solution.py:20
  273.6 36.9 %collective-permute-start.1 = (bf16[320,1024]{1,0:T(8,128)(2,1)S(1)}, bf16[320,1024]{1,0:T(8,128)(2,1)S(1)}, u32[]{:S(2)}, u32[]{:S(2)}) collective-permute-start(bf16[320,1024]{1,0:T(8,128)(2,1)S(1)} %get-tuple-element.49), channel_id=1, source_target_pairs={{0,2},{1,3},{2,0},{3,1},{4,6},{5,7},{6,4},{7,5},{8,10},{9,11},{10,... | collective-permute-start | bytes 1966088 | tf_op jit(solution)/shard_map/ppermute | solution.py:20
  279.8 47.2 %collective-permute-start = (bf16[320,1024]{1,0:T(8,128)(2,1)S(1)}, bf16[320,1024]{1,0:T(8,128)(2,1)S(1)}, u32[]{:S(2)}, u32[]{:S(2)}) collective-permute-start(bf16[320,1024]{1,0:T(8,128)(2,1)S(1)} %get-tuple-element.50), channel_id=1, source_target_pairs={{0,1},{1,2},{2,3},{3,0},{4,5},{5,6},{6,7},{7,4},{8,9},{9,10},{10,1... | collective-permute-start | bytes 1966088 | tf_op jit(solution)/shard_map/ppermute | solution.py:20
  334.8 30.7 %copy-start.16 = (bf16[1280,512]{1,0:T(8,128)(2,1)}, bf16[1280,512]{1,0:T(8,128)(2,1)S(1)}, u32[]{:S(2)}) copy-start(bf16[1280,512]{1,0:T(8,128)(2,1)S(1)} %multiply_convert_fusion) | copy-start | bytes 3932164
  334.8 5.3 copy-start.9
  334.9 5.3 copy-start.10
  334.9 5.3 copy-start.11
  337.4 17.0 %collective-permute-start.14 = (bf16[320,512]{1,0:T(8,128)(2,1)S(1)}, bf16[320,512]{1,0:T(8,128)(2,1)S(1)}, u32[]{:S(2)}, u32[]{:S(2)}) collective-permute-start(bf16[320,512]{1,0:T(8,128)(2,1)S(1)} %get-tuple-element.60), channel_id=1, source_target_pairs={{0,1},{1,2},{2,3},{3,0},{4,5},{5,6},{6,7},{7,4},{8,9},{9,10},{10,1... | collective-permute-start | bytes 983048 | tf_op jit(solution)/shard_map/ppermute | solution.py:20
  337.4 16.9 %collective-permute-start.13 = (bf16[320,512]{1,0:T(8,128)(2,1)S(1)}, bf16[320,512]{1,0:T(8,128)(2,1)S(1)}, u32[]{:S(2)}, u32[]{:S(2)}) collective-permute-start(bf16[320,512]{1,0:T(8,128)(2,1)S(1)} %get-tuple-element.61), channel_id=1, source_target_pairs={{0,2},{1,3},{2,0},{3,1},{4,6},{5,7},{6,4},{7,5},{8,10},{9,11},{10,... | collective-permute-start | bytes 983048 | tf_op jit(solution)/shard_map/ppermute | solution.py:20
  338.0 16.8 %collective-permute-start.12 = (bf16[320,512]{1,0:T(8,128)(2,1)S(1)}, bf16[320,512]{1,0:T(8,128)(2,1)S(1)}, u32[]{:S(2)}, u32[]{:S(2)}) collective-permute-start(bf16[320,512]{1,0:T(8,128)(2,1)S(1)} %get-tuple-element.62), channel_id=1, source_target_pairs={{0,3},{1,0},{2,1},{3,2},{4,7},{5,4},{6,5},{7,6},{8,11},{9,8},{10,9... | collective-permute-start | bytes 983048 | tf_op jit(solution)/shard_map/ppermute | solution.py:20
  340.4 16.9 %copy-start = (bf16[1024,1280]{0,1:T(8,128)(2,1)}, bf16[1024,1280]{0,1:T(8,128)(2,1)S(1)}, u32[]{:S(2)}) copy-start(bf16[1024,1280]{0,1:T(8,128)(2,1)S(1)} %pad_maximum_fusion.4) | copy-start | bytes 7864324
  357.4 48.9 %all-to-all-start.4 = ((bf16[64,16,512]{2,1,0:T(8,128)(2,1)}), bf16[64,16,512]{2,1,0:T(8,128)(2,1)S(1)}, u32[]{:S(2)}, u32[]{:S(2)}) async-start(bf16[64,16,512]{2,1,0:T(8,128)(2,1)} %bitcast.18), calls=%async_computation.4 | async-start | bytes 2097152 | tf_op jit(solution)/shard_map/all_to_all | solution.py:119
  368.6 17.2 %collective-permute-start.23 = (bf16[320,1024]{1,0:T(8,128)(2,1)S(1)}, bf16[320,1024]{1,0:T(8,128)(2,1)S(1)}, u32[]{:S(2)}, u32[]{:S(2)}) collective-permute-start(bf16[320,1024]{1,0:T(8,128)(2,1)S(1)} %get-tuple-element.44), channel_id=1, source_target_pairs={{0,1},{1,2},{2,3},{3,0},{4,5},{5,6},{6,7},{7,4},{8,9},{9,10},{10,1... | collective-permute-start | bytes 1966088 | tf_op jit(solution)/shard_map/ppermute | solution.py:20
  368.7 31.8 %collective-permute-start.22 = (bf16[320,1024]{1,0:T(8,128)(2,1)S(1)}, bf16[320,1024]{1,0:T(8,128)(2,1)S(1)}, u32[]{:S(2)}, u32[]{:S(2)}) collective-permute-start(bf16[320,1024]{1,0:T(8,128)(2,1)S(1)} %get-tuple-element.45), channel_id=1, source_target_pairs={{0,2},{1,3},{2,0},{3,1},{4,6},{5,7},{6,4},{7,5},{8,10},{9,11},{10,... | collective-permute-start | bytes 1966088 | tf_op jit(solution)/shard_map/ppermute | solution.py:20
  371.9 28.5 %collective-permute-start.21 = (bf16[320,1024]{1,0:T(8,128)(2,1)S(1)}, bf16[320,1024]{1,0:T(8,128)(2,1)S(1)}, u32[]{:S(2)}, u32[]{:S(2)}) collective-permute-start(bf16[320,1024]{1,0:T(8,128)(2,1)S(1)} %get-tuple-element.46), channel_id=1, source_target_pairs={{0,3},{1,0},{2,1},{3,2},{4,7},{5,4},{6,5},{7,6},{8,11},{9,8},{10,9... | collective-permute-start | bytes 1966088 | tf_op jit(solution)/shard_map/ppermute | solution.py:20
  406.3 60.9 %all-to-all-start.7 = ((bf16[64,16,1024]{2,1,0:T(8,128)(2,1)}), bf16[64,16,1024]{2,1,0:T(8,128)(2,1)S(1)}, u32[]{:S(2)}, u32[]{:S(2)}) async-start(bf16[64,16,1024]{2,1,0:T(8,128)(2,1)} %bitcast.94), calls=%async_computation.7 | async-start | bytes 4194304 | tf_op jit(solution)/shard_map/all_to_all | solution.py:119
  420.9 17.1 %collective-permute-start.20 = (bf16[320,1024]{1,0:T(8,128)(2,1)S(1)}, bf16[320,1024]{1,0:T(8,128)(2,1)S(1)}, u32[]{:S(2)}, u32[]{:S(2)}) collective-permute-start(bf16[320,1024]{1,0:T(8,128)(2,1)S(1)} %get-tuple-element.40), channel_id=1, source_target_pairs={{0,1},{1,2},{2,3},{3,0},{4,5},{5,6},{6,7},{7,4},{8,9},{9,10},{10,1... | collective-permute-start | bytes 1966088 | tf_op jit(solution)/shard_map/ppermute | solution.py:20
  420.9 31.9 %collective-permute-start.19 = (bf16[320,1024]{1,0:T(8,128)(2,1)S(1)}, bf16[320,1024]{1,0:T(8,128)(2,1)S(1)}, u32[]{:S(2)}, u32[]{:S(2)}) collective-permute-start(bf16[320,1024]{1,0:T(8,128)(2,1)S(1)} %get-tuple-element.41), channel_id=1, source_target_pairs={{0,2},{1,3},{2,0},{3,1},{4,6},{5,7},{6,4},{7,5},{8,10},{9,11},{10,... | collective-permute-start | bytes 1966088 | tf_op jit(solution)/shard_map/ppermute | solution.py:20
  424.5 28.4 %collective-permute-start.18 = (bf16[320,1024]{1,0:T(8,128)(2,1)S(1)}, bf16[320,1024]{1,0:T(8,128)(2,1)S(1)}, u32[]{:S(2)}, u32[]{:S(2)}) collective-permute-start(bf16[320,1024]{1,0:T(8,128)(2,1)S(1)} %get-tuple-element.42), channel_id=1, source_target_pairs={{0,3},{1,0},{2,1},{3,2},{4,7},{5,4},{6,5},{7,6},{8,11},{9,8},{10,9... | collective-permute-start | bytes 1966088 | tf_op jit(solution)/shard_map/ppermute | solution.py:20
  467.2 57.0 %all-to-all-start.6 = ((bf16[64,16,1024]{2,1,0:T(8,128)(2,1)}), bf16[64,16,1024]{2,1,0:T(8,128)(2,1)}, u32[]{:S(2)}, u32[]{:S(2)}) async-start(bf16[64,16,1024]{2,1,0:T(8,128)(2,1)} %bitcast.93), calls=%async_computation.6 | async-start | bytes 4194304 | tf_op jit(solution)/shard_map/all_to_all | solution.py:119
  478.2 17.3 %collective-permute-start.17 = (bf16[320,1024]{1,0:T(8,128)(2,1)S(1)}, bf16[320,1024]{1,0:T(8,128)(2,1)S(1)}, u32[]{:S(2)}, u32[]{:S(2)}) collective-permute-start(bf16[320,1024]{1,0:T(8,128)(2,1)S(1)} %get-tuple-element.36), channel_id=1, source_target_pairs={{0,1},{1,2},{2,3},{3,0},{4,5},{5,6},{6,7},{7,4},{8,9},{9,10},{10,1... | collective-permute-start | bytes 1966088 | tf_op jit(solution)/shard_map/ppermute | solution.py:20
  478.2 32.1 %collective-permute-start.16 = (bf16[320,1024]{1,0:T(8,128)(2,1)S(1)}, bf16[320,1024]{1,0:T(8,128)(2,1)S(1)}, u32[]{:S(2)}, u32[]{:S(2)}) collective-permute-start(bf16[320,1024]{1,0:T(8,128)(2,1)S(1)} %get-tuple-element.37), channel_id=1, source_target_pairs={{0,2},{1,3},{2,0},{3,1},{4,6},{5,7},{6,4},{7,5},{8,10},{9,11},{10,... | collective-permute-start | bytes 1966088 | tf_op jit(solution)/shard_map/ppermute | solution.py:20
  481.8 28.6 %collective-permute-start.15 = (bf16[320,1024]{1,0:T(8,128)(2,1)S(1)}, bf16[320,1024]{1,0:T(8,128)(2,1)S(1)}, u32[]{:S(2)}, u32[]{:S(2)}) collective-permute-start(bf16[320,1024]{1,0:T(8,128)(2,1)S(1)} %get-tuple-element.38), channel_id=1, source_target_pairs={{0,3},{1,0},{2,1},{3,2},{4,7},{5,4},{6,5},{7,6},{8,11},{9,8},{10,9... | collective-permute-start | bytes 1966088 | tf_op jit(solution)/shard_map/ppermute | solution.py:20
  524.2 56.8 %all-to-all-start.5 = ((bf16[64,16,1024]{2,1,0:T(8,128)(2,1)}), bf16[64,16,1024]{2,1,0:T(8,128)(2,1)}, u32[]{:S(2)}, u32[]{:S(2)}) async-start(bf16[64,16,1024]{2,1,0:T(8,128)(2,1)} %bitcast.95), calls=%async_computation.5 | async-start | bytes 4194304 | tf_op jit(solution)/shard_map/all_to_all | solution.py:119
  (9 other events, 13.1 us)
